TPU v7x, 128 devices: a whole 4x4x4 slice. The times are simulated.
128 devices in a mesh: gx: 16 (over x, y_hi, core), gy: 8 (over y_lo, z).
Axes of the slice: x: 4, y: 4 (y_hi: 2, y_lo: 2; y = y_hi * 2 + y_lo), z: 4, core: 2. Of those that a mesh axis runs over, the one named last changes fastest.
Arguments:
- right_side: float32 [512, 256, 512], P('gx', 'gy'), may hold values from -24 to 24
- alpha_coef: float32 [512, 256, 512], P('gx', 'gy'), may hold values from 0.05 to 0.5
- face_coef: float32 [3, 512, 256, 512], P(None, 'gx', 'gy'), may hold values from 0.25 to 4
- owner_map: int32 [8, 256], P('gy'), may hold values from 0 to 15, as said below
Outputs:
- solution: float32 [512, 256, 512], P('gx', 'gy')
- coarse_residual: float32 [256, 128, 256], P('gx', 'gy')
- coarse_coef: float32 [4, 256, 128, 256], P(None, 'gx', 'gy')
Inputs may be any that keep to these rules, and one draw needn't show every extreme that they name: `owner_map`: each row's tiles are cut by recursive bisection into boxes of 4 x 4 tiles, one box to each owner; every device that sends to an owner sends it exactly 4 tiles.
All inputs are finite; a program needn't handle non-finite values.
Results may differ from a plain program's by a relative error of at most 0.00002.
Values sent between devices are 32-bit elements; how exact they have to be, the bound alone decides.
A program may use at most 192 MiB of HBM per device.

v0:
```python
import jax
import jax.numpy as jnp
from jax import lax
from jax.sharding import PartitionSpec as P

SIDE = 4
ITERS = 4


cheb_high = 2.0
cheb_low = 0.25


def padded_2(cells, sides, width):
    for axis, dim in sides:
        count = lax.axis_size(axis)
        ends = count - 1
        head = lax.slice_in_dim(cells, 0, width, axis=dim)
        tail = lax.slice_in_dim(cells, cells.shape[dim] - width, cells.shape[dim], axis=dim)
        cells = jnp.concatenate(
            [
                lax.ppermute(tail, axis, [(i, (i + 1) % count) for i in range(ends)]),
                cells,
                lax.ppermute(head, axis, [((i + 1) % count, i) for i in range(ends)]),
            ],
            axis=dim,
        )
    return cells


def passed_along(block, axis, distance):
    devices = range(lax.axis_size(axis))
    route = [(i - distance, i) for i in devices if i - distance in devices]
    return lax.ppermute(block, axis, route)


def shift_lower(field):
    return jnp.concatenate([jnp.zeros_like(field[..., :1]), field[..., :-1]], axis=-1)


def shift_upper(field):
    return jnp.concatenate([field[..., 1:], jnp.zeros_like(field[..., :1])], axis=-1)


def apply_operator(padded, alpha_inner, faces_padded):
    center = padded[1:-1, 1:-1]
    face_x = faces_padded[0, 1:-1, 1:-1]
    face_xu = faces_padded[0, 2:, 1:-1]
    face_y = faces_padded[1, 1:-1, 1:-1]
    face_yu = faces_padded[1, 1:-1, 2:]
    face_z = faces_padded[2, 1:-1, 1:-1]
    face_zu = shift_upper(face_z)
    result = alpha_inner * center
    result = result + face_x * (center - padded[:-2, 1:-1]) + face_xu * (center - padded[2:, 1:-1])
    result = result + face_y * (center - padded[1:-1, :-2]) + face_yu * (center - padded[1:-1, 2:])
    result = (
        result + face_z * (center - shift_lower(center)) + face_zu * (center - shift_upper(center))
    )
    return result


def diagonal_of(alpha_inner, faces_padded):
    face_x = faces_padded[0, 1:-1, 1:-1]
    face_xu = faces_padded[0, 2:, 1:-1]
    face_y = faces_padded[1, 1:-1, 1:-1]
    face_yu = faces_padded[1, 1:-1, 2:]
    face_z = faces_padded[2, 1:-1, 1:-1]
    return alpha_inner + face_x + face_xu + face_y + face_yu + face_z + shift_upper(face_z)


def chebyshev_constants():
    theta_mid = (cheb_high + cheb_low) / 2.0
    delta_half = (cheb_high - cheb_low) / 2.0
    return (theta_mid, delta_half, theta_mid / delta_half)


def field_with_rim(field):
    return padded_2(field, (("gx", 0), ("gy", 1)), 1)


def faces_with_next(face_coef):
    next_x = passed_along(face_coef[0, :1], "gx", -1)
    next_y = passed_along(face_coef[1, :, :1], "gy", -1)
    padded_x = jnp.pad(jnp.concatenate([face_coef[0], next_x], axis=0), ((1, 0), (1, 1), (0, 0)))
    padded_y = jnp.pad(jnp.concatenate([face_coef[1], next_y], axis=1), ((1, 1), (1, 0), (0, 0)))
    padded_z = jnp.pad(face_coef[2], ((1, 1), (1, 1), (0, 0)))
    return jnp.stack([padded_x, padded_y, padded_z], axis=0)


def smooth_each(right_side, alpha_coef, face_coef):
    theta_mid, delta_half, sigma_ratio = chebyshev_constants()
    faces_padded = faces_with_next(face_coef)
    inverse = 1.0 / diagonal_of(alpha_coef, faces_padded)
    solution = inverse * right_side / theta_mid
    update = solution
    rho_prev = 1.0 / sigma_ratio
    for _ in range(ITERS - 1):
        residual = right_side - apply_operator(field_with_rim(solution), alpha_coef, faces_padded)
        rho_next = 1.0 / (2.0 * sigma_ratio - rho_prev)
        update = rho_next * rho_prev * update + 2.0 * rho_next / delta_half * inverse * residual
        solution = solution + update
        rho_prev = rho_next
    residual = right_side - apply_operator(field_with_rim(solution), alpha_coef, faces_padded)
    return (solution, residual)


def pair_sum_z(field):
    return field[..., 0::2] + field[..., 1::2]


def split_major(field):
    return field.reshape(field.shape[0] // 2, 2, field.shape[1] // 2, 2, field.shape[2])


def average_cells(field):
    return jnp.sum(split_major(pair_sum_z(field)), axis=(1, 3)) * 0.125


def average_faces(faces):
    along_x = jnp.sum(split_major(pair_sum_z(faces[0]))[:, 0], axis=2) * 0.25
    along_y = jnp.sum(split_major(pair_sum_z(faces[1]))[:, :, :, 0], axis=1) * 0.25
    along_z = jnp.sum(split_major(faces[2][..., 0::2]), axis=(1, 3)) * 0.25
    return [along_x, along_y, along_z]


def coarse_tiles(coarse, tiles_dev):
    half_cells = coarse.shape[0]
    shaped = coarse.reshape(coarse.shape[0], coarse.shape[1], tiles_dev, half_cells)
    return shaped.transpose(2, 1, 0, 3).reshape(tiles_dev, half_cells, half_cells * half_cells)


def send_slots(owner_row, device_x, devices_x, tiles_dev):
    mine = lax.dynamic_slice_in_dim(owner_row, device_x * tiles_dev, tiles_dev)
    tile_index = jnp.arange(tiles_dev, dtype=jnp.int32)
    earlier = tile_index[None, :] < tile_index[:, None]
    same_owner = mine[None, :] == mine[:, None]
    order_rank = jnp.sum((earlier & same_owner).astype(jnp.int32), axis=1)
    slot_index = jnp.arange(devices_x * SIDE, dtype=jnp.int32)
    target = slot_index // SIDE
    within = slot_index % SIDE
    matches = (mine[None, :] == target[:, None]) & (order_rank[None, :] == within[:, None])
    picked = jnp.sum(jnp.where(matches, tile_index[None, :], 0), axis=1)
    used = jnp.any(matches, axis=1)
    return (picked, used)


def receive_slots(owner_row, device_x, tiles_dev):
    owned = owner_row == device_x
    tile_ids = jnp.arange(owner_row.shape[0], dtype=jnp.int32)
    position = jnp.cumsum(owned.astype(jnp.int32)) - 1
    wanted = jnp.arange(tiles_dev, dtype=jnp.int32)
    selected = owned[None, :] & (position[None, :] == wanted[:, None])
    chosen_id = jnp.sum(jnp.where(selected, tile_ids[None, :], 0), axis=1)
    source = chosen_id // tiles_dev
    before = jnp.sum(
        (owned[None, :] & (tile_ids[None, :] < (source * tiles_dev)[:, None])).astype(jnp.int32),
        axis=1,
    )
    return source * SIDE + wanted - before


def pack_tiles(tiles, picked, used):
    gathered = jnp.take(tiles, picked, axis=1)
    return jnp.where(used[None, :, None, None], gathered, 0.0)


def local(right_side, alpha_coef, face_coef, owner_map):
    cells = right_side.shape[0]
    tiles_dev = right_side.shape[2] // cells
    devices_x = lax.axis_size("gx")
    device_x = lax.axis_index("gx")
    owner_row = owner_map[0]
    picked, used = send_slots(owner_row, device_x, devices_x, tiles_dev)
    arrival = receive_slots(owner_row, device_x, tiles_dev)
    fields = [average_cells(alpha_coef)] + average_faces(face_coef)
    coef_tiles = jnp.stack([coarse_tiles(field, tiles_dev) for field in fields], axis=0)
    coef_send = pack_tiles(coef_tiles, picked, used)
    solution, residual = smooth_each(right_side, alpha_coef, face_coef)
    residual_tiles = coarse_tiles(average_cells(residual), tiles_dev)[None]
    residual_send = pack_tiles(residual_tiles, picked, used)
    residual_back, coef_back = (
        lax.all_to_all(residual_send, "gx", split_axis=1, concat_axis=1, tiled=True),
        lax.all_to_all(coef_send, "gx", split_axis=1, concat_axis=1, tiled=True),
    )
    coarse_residual = jnp.take(residual_back[0], arrival, axis=0)
    coarse_coef = jnp.take(coef_back, arrival, axis=1)
    return (solution, coarse_residual, coarse_coef)


def solution(mesh):
    return jax.shard_map(
        local,
        mesh=mesh,
        in_specs=(
            P("gx", "gy", None),
            P("gx", "gy", None),
            P(None, "gx", "gy", None),
            P("gy", None),
        ),
        out_specs=(P("gx", "gy", None), P("gx", "gy", None), P(None, "gx", "gy", None)),
        check_vma=False,
    )
```

profile of v0, /device:TPU:29, one launch (start us, length us, event | category | flops | bytes accessed | tf_op | source)
XLA Modules:
  0.0 653.5 jit_solution(1038996379201672666)
XLA Ops:
  1.7 2.6 collective-permute-start
  5.4 5.8 collective-permute-start.1
  11.3 36.5 %slice.292 = f32[32,32,256]{2,1,0:T(8,128)} slice(f32[32,32,512]{2,1,0:T(8,128)} %param.5), slice={[0:32:1], [0:32:1], [1:512:2]} | slice | bytes 2097152 | tf_op jit(solution)/shard_map/slice | solution.py:108
  47.7 35.6 %slice.291 = f32[32,32,256]{2,1,0:T(8,128)} slice(f32[32,32,512]{2,1,0:T(8,128)S(1)} %copy-done.6), slice={[0:32:1], [0:32:1], [0:512:2]} | slice | bytes 2097152 | tf_op jit(solution)/shard_map/slice | solution.py:108
  83.4 6.0 fusion.87
  90.6 35.3 %slice.294 = f32[32,32,256]{2,0,1:T(8,128)S(1)} slice(f32[32,32,512]{2,0,1:T(8,128)S(1)} %bitcast.155), slice={[0:32:1], [0:32:1], [1:512:2]} | slice | bytes 2097152 | tf_op jit(solution)/shard_map/slice | solution.py:108
  125.9 36.0 %slice.293 = f32[32,32,256]{2,0,1:T(8,128)} slice(f32[32,32,512]{2,0,1:T(8,128)S(1)} %bitcast.156), slice={[0:32:1], [0:32:1], [0:512:2]} | slice | bytes 2097152 | tf_op jit(solution)/shard_map/slice | solution.py:108
  173.0 4.0 copy_bitcast_fusion
  184.4 7.7 %broadcast_multiply_fusion = (f32[32,32,512]{2,0,1:T(8,128)S(1)}, f32[32,32,512]{2,0,1:T(8,128)}) fusion(f32[32,32,512]{2,1,0:T(8,128)S(1)} %copy-done.14, f32[32,32,511]{2,0,1:T(8,128)S(1)} %slice.313, f32[1,34,34,512]{3,1,2,0:T(8,128)S(1)} %pad_bitcast_fusion, f32[1,34,34,512]{3,1,2,0:T(8,128)S(1)} %fusion.2, f32[1,34,34,512]{3,1,2,0:T(8,128)S(1)} %fusion.3, ...), kind=kLoop, calls=%fused_computation.132 | loop fusion | flops 4718592 | bytes 20967424 | tf_op jit(solution)/shard_map/div | solution.py:94
  192.2 6.3 collective-permute-start.2
  200.4 6.0 collective-permute-done.3
  208.6 5.5 collective-permute-start.5
  214.0 2.7 fusion.95
  216.8 15.2 %fusion.76 = (f32[32,32,512]{2,0,1:T(8,128)}, f32[32,32,512]{2,0,1:T(8,128)}) fusion(f32[32,32,512]{2,0,1:T(8,128)} %get-tuple-element.28, f32[32,32,512]{2,0,1:T(8,128)} %copy-done.12, f32[32,32,511]{2,0,1:T(8,128)} %get-tuple-element.55, f32[32,32,511]{2,0,1:T(8,128)} %get-tuple-element.54, f32[34,1,512]{2,0,1:T(8,128)S(1)} %collective-permute-done.5, ...), kind=kLoop, calls=%fused_computation.133 | loop fusion | flops 21495808 | bytes 29618176 | tf_op jit(solution)/shard_map/add | solution.py:101
  237.7 36.5 %slice.299 = f32[32,32,256]{2,0,1:T(8,128)} slice(f32[32,32,512]{2,0,1:T(8,128)} %copy-done.20), slice={[0:32:1], [0:32:1], [0:512:2]} | slice | bytes 2097152 | tf_op jit(solution)/shard_map/slice | solution.py:122
  274.2 2.9 reshape.222
  282.1 6.0 collective-permute-start.9
  288.1 5.1 fusion.93
  293.2 15.0 %fusion.83 = (f32[32,32,512]{2,0,1:T(8,128)}, f32[32,32,512]{2,0,1:T(8,128)}) fusion(f32[32,32,512]{2,0,1:T(8,128)} %get-tuple-element.25, f32[32,32,511]{2,0,1:T(8,128)} %get-tuple-element.51, f32[32,32,511]{2,0,1:T(8,128)} %get-tuple-element.50, f32[34,1,512]{2,0,1:T(8,128)S(1)} %collective-permute-done.9, f32[1,32,512]{2,0,1:T(1,128)S(1)} %collective-permute-done.7, ...), kind=kLoop, calls=%fused_computation.199 | loop fusion | flops 20971520 | bytes 29618176 | tf_op jit(solution)/shard_map/add | solution.py:101
  309.7 6.6 %collective-permute-start.10 = (f32[1,32,512]{2,0,1:T(1,128)S(1)}, f32[1,32,512]{2,0,1:T(1,128)S(1)}, u32[]{:S(2)}, u32[]{:S(2)}) collective-permute-start(f32[1,32,512]{2,0,1:T(1,128)S(1)} %get-tuple-element.46), channel_id=1, source_target_pairs={{0,8},{8,16},{16,24},{24,32},{32,40},{40,48},{48,56},{56,64},{64,7... | collective-permute-start | bytes 196616 | tf_op jit(solution)/shard_map/ppermute | solution.py:22
  318.3 6.0 collective-permute-done.11
  327.1 5.5 collective-permute-start.13
  332.6 2.8 fusion.90
  335.4 13.9 %fusion.29 = f32[32,32,512]{2,0,1:T(8,128)S(1)} fusion(f32[32,32,512]{2,0,1:T(8,128)} %get-tuple-element.23, f32[34,1,512]{2,0,1:T(8,128)S(1)} %collective-permute-done.13, f32[1,32,512]{2,0,1:T(1,128)S(1)} %collective-permute-done.11, f32[1,32,512]{2,0,1:T(1,128)S(1)} %collective-permute-done.10, f32[34,1,512]{2,0,1:T(8,128)S(1)} %collective-permute-done.12, ...), kind=kLoop, calls=%fused_computation.50 | loop fusion | flops 20971520 | bytes 27521024 | tf_op jit(solution)/shard_map/add | solution.py:101
  353.9 6.0 collective-permute-done.15
  361.9 5.7 collective-permute-start.17
  367.6 2.8 fusion.88
  370.5 12.2 %fusion.11 = f32[32,32,512]{2,0,1:T(8,128)} fusion(f32[32,32,512]{2,0,1:T(8,128)S(1)} %fusion.29, f32[34,1,512]{2,0,1:T(8,128)S(1)} %collective-permute-done.17, f32[1,32,512]{2,0,1:T(1,128)S(1)} %collective-permute-done.15, f32[1,32,512]{2,0,1:T(1,128)S(1)} %collective-permute-done.14, f32[34,1,512]{2,0,1:T(8,128)S(1)} %collective-permute-done.16, ...), kind=kLoop, calls=%fused_computation.24 | loop fusion | flops 14680064 | bytes 25423872 | tf_op jit(solution)/shard_map/sub | solution.py:103
  382.7 36.0 %slice.290 = f32[32,32,256]{2,0,1:T(8,128)S(1)} slice(f32[32,32,512]{2,0,1:T(8,128)} %fusion.11), slice={[0:32:1], [0:32:1], [1:512:2]} | slice | bytes 2097152 | tf_op jit(solution)/shard_map/slice | solution.py:108
  418.8 35.8 %slice.289 = f32[32,32,256]{2,0,1:T(8,128)} slice(f32[32,32,512]{2,0,1:T(8,128)S(1)} %copy-done.21), slice={[0:32:1], [0:32:1], [0:512:2]} | slice | bytes 2097152 | tf_op jit(solution)/shard_map/slice | solution.py:108
  458.2 2.6 copy.117
  465.0 7.0 %all-to-all-start = ((f32[1,64,16,256]{3,2,0,1:T(8,128)}), f32[1,64,16,256]{3,2,0,1:T(8,128)}, u32[]{:S(2)}, u32[]{:S(2)}) async-start(f32[1,64,16,256]{3,2,0,1:T(8,128)} %fusion.75), calls=%async_computation | async-start | bytes 2097152 | tf_op jit(solution)/shard_map/all_to_all | solution.py:182
  472.7 35.1 %slice.297 = f32[32,32,256]{2,0,1:T(8,128)S(1)} slice(f32[32,32,512]{2,0,1:T(8,128)S(1)} %copy-done.19), slice={[0:32:1], [0:32:1], [1:512:2]} | slice | bytes 2097152 | tf_op jit(solution)/shard_map/slice | solution.py:108
  507.8 35.6 %slice.296 = f32[32,32,256]{2,0,1:T(8,128)} slice(f32[32,32,512]{2,0,1:T(8,128)S(1)} %copy-done.19), slice={[0:32:1], [0:32:1], [0:512:2]} | slice | bytes 2097152 | tf_op jit(solution)/shard_map/slice | solution.py:108
  545.2 2.6 copy.121
  547.8 3.1 stack_reshape.12
  551.7 2.6 copy.123
  554.3 3.3 stack_reshape.13
  560.0 2.6 copy.125
  565.6 2.6 copy.127
  568.2 2.5 stack_reshape.15
  570.8 2.8 gather_fusion.2
  573.6 4.7 select_bitcast_fusion
  578.3 7.4 %all-to-all-start.1 = ((f32[4,64,16,256]{3,2,0,1:T(8,128)}), f32[4,64,16,256]{3,2,0,1:T(8,128)}, u32[]{:S(2)}, u32[]{:S(2)}) async-start(f32[4,64,16,256]{3,2,0,1:T(8,128)} %select_bitcast_fusion), calls=%async_computation.1 | async-start | bytes 8388608 | tf_op jit(solution)/shard_map/all_to_all | solution.py:183
  586.7 2.5 copy.129
  591.8 52.5 %all-to-all-done.1 = f32[4,64,16,256]{3,2,0,1:T(8,128)} async-done(((f32[4,64,16,256]{3,2,0,1:T(8,128)}), f32[4,64,16,256]{3,2,0,1:T(8,128)}, u32[]{:S(2)}, u32[]{:S(2)}) %all-to-all-start.1) | async-done | bytes 4194336 | tf_op jit(solution)/shard_map/all_to_all | solution.py:183
  644.3 4.8 copy.128
  649.1 2.8 gather_fusion.3
  (161 shorter events, 70.5 us)
Async XLA Ops:
  0.6 47.1 %copy-start.6 = (f32[32,32,512]{2,1,0:T(8,128)S(1)}, f32[32,32,512]{2,1,0:T(8,128)}, u32[]{:S(2)}) copy-start(f32[32,32,512]{2,1,0:T(8,128)} %param.5) | copy-start | bytes 6291460
  1.7 177.8 %collective-permute-start = (f32[1,32,512]{2,0,1:T(1,128)S(1)}, f32[1,32,512]{2,0,1:T(1,128)S(1)}, u32[]{:S(2)}, u32[]{:S(2)}) collective-permute-start(f32[1,32,512]{2,0,1:T(1,128)S(1)} %bitcast.163), channel_id=1, source_target_pairs={{8,0},{16,8},{24,16},{32,24},{40,32},{48,40},{56,48},{64,56},{72,6... | collective-permute-start | bytes 196616 | tf_op jit(solution)/shard_map/ppermute | solution.py:34
  5.4 176.8 %collective-permute-start.1 = (f32[32,1,512]{2,0,1:T(8,128)S(1)}, f32[32,1,512]{2,0,1:T(8,128)S(1)}, u32[]{:S(2)}, u32[]{:S(2)}) collective-permute-start(f32[32,1,512]{2,0,1:T(8,128)S(1)} %bitcast.164), channel_id=1, source_target_pairs={{1,0},{2,1},{3,2},{4,3},{5,4},{6,5},{7,6},{9,8},{10,9},{11,10},{12... | collective-permute-start | bytes 196616 | tf_op jit(solution)/shard_map/ppermute | solution.py:34
  90.6 71.4 %copy-start.16 = (f32[1,32,32,512]{3,1,2,0:T(8,128)}, f32[1,32,32,512]{3,1,2,0:T(8,128)S(1)}, u32[]{:S(2)}) copy-start(f32[1,32,32,512]{3,1,2,0:T(8,128)S(1)} %copy.158) | copy-start | bytes 6291460
  90.6 71.4 %copy-start.29 = (s32[1,256]{1,0:T(1,128)S(1)}, s32[1,256]{1,0:T(1,128)}, u32[]{:S(2)}) copy-start(s32[1,256]{1,0:T(1,128)} %param.7) | copy-start | bytes 3076
  163.9 4.5 copy-start.23
  169.6 3.5 copy-start.22
  177.1 5.1 copy-start.18
  178.4 38.3 %copy-start.2 = (f32[1,34,34,512]{3,1,2,0:T(8,128)}, f32[1,34,34,512]{3,1,2,0:T(8,128)S(1)}, u32[]{:S(2)}) copy-start(f32[1,34,34,512]{3,1,2,0:T(8,128)S(1)} %pad_bitcast_fusion) | copy-start | bytes 7102468
  178.8 2.9 copy-start.17
  179.4 37.4 %copy-start.9 = (f32[32,32,511]{2,0,1:T(8,128)}, f32[32,32,511]{2,0,1:T(8,128)S(1)}, u32[]{:S(2)}) copy-start(f32[32,32,511]{2,0,1:T(8,128)S(1)} %slice.313) | copy-start | bytes 6279172
  182.2 2.2 copy-start.14
  184.4 32.4 %copy-start = (f32[1,34,34,512]{3,1,2,0:T(8,128)}, f32[1,34,34,512]{3,1,2,0:T(8,128)S(1)}, u32[]{:S(2)}) copy-start(f32[1,34,34,512]{3,1,2,0:T(8,128)S(1)} %fusion.2) | copy-start | bytes 7102468
  192.1 24.7 %copy-start.12 = (f32[32,32,512]{2,0,1:T(8,128)}, f32[32,32,512]{2,0,1:T(8,128)S(1)}, u32[]{:S(2)}) copy-start(f32[32,32,512]{2,0,1:T(8,128)S(1)} %get-tuple-element.27) | copy-start | bytes 6291460
  192.2 8.2 %collective-permute-start.2 = (f32[1,32,512]{2,0,1:T(1,128)S(1)}, f32[1,32,512]{2,0,1:T(1,128)S(1)}, u32[]{:S(2)}, u32[]{:S(2)}) collective-permute-start(f32[1,32,512]{2,0,1:T(1,128)S(1)} %get-tuple-element.52), channel_id=1, source_target_pairs={{0,8},{8,16},{16,24},{24,32},{32,40},{40,48},{48,56},{56,64},{64,7... | collective-permute-start | bytes 196616 | tf_op jit(solution)/shard_map/ppermute | solution.py:22
  198.5 8.0 %collective-permute-start.3 = (f32[1,32,512]{2,0,1:T(1,128)S(1)}, f32[1,32,512]{2,0,1:T(1,128)S(1)}, u32[]{:S(2)}, u32[]{:S(2)}) collective-permute-start(f32[1,32,512]{2,0,1:T(1,128)S(1)} %get-tuple-element.53), channel_id=1, source_target_pairs={{8,0},{16,8},{24,16},{32,24},{40,32},{48,40},{56,48},{64,56},{72,6... | collective-permute-start | bytes 196616 | tf_op jit(solution)/shard_map/ppermute | solution.py:24
  206.5 10.3 %collective-permute-start.4 = (f32[34,1,512]{2,0,1:T(8,128)S(1)}, f32[34,1,512]{2,0,1:T(8,128)S(1)}, u32[]{:S(2)}, u32[]{:S(2)}) collective-permute-start(f32[34,1,512]{2,0,1:T(8,128)S(1)} %get-tuple-element.38), channel_id=1, source_target_pairs={{0,1},{1,2},{2,3},{3,4},{4,5},{5,6},{6,7},{8,9},{9,10},{10,11},{11... | collective-permute-start | bytes 208904 | tf_op jit(solution)/shard_map/ppermute | solution.py:22
  208.6 8.2 %collective-permute-start.5 = (f32[34,1,512]{2,0,1:T(8,128)S(1)}, f32[34,1,512]{2,0,1:T(8,128)S(1)}, u32[]{:S(2)}, u32[]{:S(2)}) collective-permute-start(f32[34,1,512]{2,0,1:T(8,128)S(1)} %get-tuple-element.39), channel_id=1, source_target_pairs={{1,0},{2,1},{3,2},{4,3},{5,4},{6,5},{7,6},{9,8},{10,9},{11,10},{12... | collective-permute-start | bytes 208904 | tf_op jit(solution)/shard_map/ppermute | solution.py:24
  233.3 45.7 %collective-permute-start.6 = (f32[1,32,512]{2,0,1:T(1,128)S(1)}, f32[1,32,512]{2,0,1:T(1,128)S(1)}, u32[]{:S(2)}, u32[]{:S(2)}) collective-permute-start(f32[1,32,512]{2,0,1:T(1,128)S(1)} %get-tuple-element.48), channel_id=1, source_target_pairs={{0,8},{8,16},{16,24},{24,32},{32,40},{40,48},{48,56},{56,64},{64,7... | collective-permute-start | bytes 196616 | tf_op jit(solution)/shard_map/ppermute | solution.py:22
  235.8 43.3 %collective-permute-start.7 = (f32[1,32,512]{2,0,1:T(1,128)S(1)}, f32[1,32,512]{2,0,1:T(1,128)S(1)}, u32[]{:S(2)}, u32[]{:S(2)}) collective-permute-start(f32[1,32,512]{2,0,1:T(1,128)S(1)} %get-tuple-element.49), channel_id=1, source_target_pairs={{8,0},{16,8},{24,16},{32,24},{40,32},{48,40},{56,48},{64,56},{72,6... | collective-permute-start | bytes 196616 | tf_op jit(solution)/shard_map/ppermute | solution.py:24
  279.1 14.1 %copy-start.10 = (f32[32,32,511]{2,0,1:T(8,128)S(1)}, f32[32,32,511]{2,0,1:T(8,128)}, u32[]{:S(2)}) copy-start(f32[32,32,511]{2,0,1:T(8,128)} %copy-done.9) | copy-start | bytes 6279172
  280.2 13.0 %collective-permute-start.8 = (f32[34,1,512]{2,0,1:T(8,128)S(1)}, f32[34,1,512]{2,0,1:T(8,128)S(1)}, u32[]{:S(2)}, u32[]{:S(2)}) collective-permute-start(f32[34,1,512]{2,0,1:T(8,128)S(1)} %get-tuple-element.36), channel_id=1, source_target_pairs={{0,1},{1,2},{2,3},{3,4},{4,5},{5,6},{6,7},{8,9},{9,10},{10,11},{11... | collective-permute-start | bytes 208904 | tf_op jit(solution)/shard_map/ppermute | solution.py:22
  282.1 11.1 %copy-start.3 = (f32[1,34,34,512]{3,1,2,0:T(8,128)S(1)}, f32[1,34,34,512]{3,1,2,0:T(8,128)}, u32[]{:S(2)}) copy-start(f32[1,34,34,512]{3,1,2,0:T(8,128)} %copy-done.2) | copy-start | bytes 7102468
  282.1 11.1 %copy-start.8 = (f32[32,32,512]{2,1,0:T(8,128)S(1)}, f32[32,32,512]{2,1,0:T(8,128)}, u32[]{:S(2)}) copy-start(f32[32,32,512]{2,1,0:T(8,128)} %param.5) | copy-start | bytes 6291460
  282.1 11.1 %collective-permute-start.9 = (f32[34,1,512]{2,0,1:T(8,128)S(1)}, f32[34,1,512]{2,0,1:T(8,128)S(1)}, u32[]{:S(2)}, u32[]{:S(2)}) collective-permute-start(f32[34,1,512]{2,0,1:T(8,128)S(1)} %get-tuple-element.37), channel_id=1, source_target_pairs={{1,0},{2,1},{3,2},{4,3},{5,4},{6,5},{7,6},{9,8},{10,9},{11,10},{12... | collective-permute-start | bytes 208904 | tf_op jit(solution)/shard_map/ppermute | solution.py:24
  288.1 5.1 copy-start.1
  308.2 24.4 %copy-start.13 = (f32[32,32,512]{2,0,1:T(8,128)S(1)}, f32[32,32,512]{2,0,1:T(8,128)}, u32[]{:S(2)}) copy-start(f32[32,32,512]{2,0,1:T(8,128)} %get-tuple-element.23) | copy-start | bytes 6291460
  309.7 8.6 %collective-permute-start.10 = (f32[1,32,512]{2,0,1:T(1,128)S(1)}, f32[1,32,512]{2,0,1:T(1,128)S(1)}, u32[]{:S(2)}, u32[]{:S(2)}) collective-permute-start(f32[1,32,512]{2,0,1:T(1,128)S(1)} %get-tuple-element.46), channel_id=1, source_target_pairs={{0,8},{8,16},{16,24},{24,32},{32,40},{40,48},{48,56},{56,64},{64,7... | collective-permute-start | bytes 196616 | tf_op jit(solution)/shard_map/ppermute | solution.py:22
  316.3 8.0 %collective-permute-start.11 = (f32[1,32,512]{2,0,1:T(1,128)S(1)}, f32[1,32,512]{2,0,1:T(1,128)S(1)}, u32[]{:S(2)}, u32[]{:S(2)}) collective-permute-start(f32[1,32,512]{2,0,1:T(1,128)S(1)} %get-tuple-element.47), channel_id=1, source_target_pairs={{8,0},{16,8},{24,16},{32,24},{40,32},{48,40},{56,48},{64,56},{72,6... | collective-permute-start | bytes 196616 | tf_op jit(solution)/shard_map/ppermute | solution.py:24
  325.2 10.2 %collective-permute-start.12 = (f32[34,1,512]{2,0,1:T(8,128)S(1)}, f32[34,1,512]{2,0,1:T(8,128)S(1)}, u32[]{:S(2)}, u32[]{:S(2)}) collective-permute-start(f32[34,1,512]{2,0,1:T(8,128)S(1)} %get-tuple-element.34), channel_id=1, source_target_pairs={{0,1},{1,2},{2,3},{3,4},{4,5},{5,6},{6,7},{8,9},{9,10},{10,11},{11... | collective-permute-start | bytes 208904 | tf_op jit(solution)/shard_map/ppermute | solution.py:22
  327.1 8.3 %collective-permute-start.13 = (f32[34,1,512]{2,0,1:T(8,128)S(1)}, f32[34,1,512]{2,0,1:T(8,128)S(1)}, u32[]{:S(2)}, u32[]{:S(2)}) collective-permute-start(f32[34,1,512]{2,0,1:T(8,128)S(1)} %get-tuple-element.35), channel_id=1, source_target_pairs={{1,0},{2,1},{3,2},{4,3},{5,4},{6,5},{7,6},{9,8},{10,9},{11,10},{12... | collective-permute-start | bytes 208904 | tf_op jit(solution)/shard_map/ppermute | solution.py:24
  349.4 21.1 %copy-start.4 = (f32[32,32,512]{2,0,1:T(8,128)}, f32[32,32,512]{2,0,1:T(8,128)S(1)}, u32[]{:S(2)}) copy-start(f32[32,32,512]{2,0,1:T(8,128)S(1)} %fusion.29) | copy-start | bytes 6291460
  349.5 4.4 collective-permute-start.14
  351.9 8.0 %collective-permute-start.15 = (f32[1,32,512]{2,0,1:T(1,128)S(1)}, f32[1,32,512]{2,0,1:T(1,128)S(1)}, u32[]{:S(2)}, u32[]{:S(2)}) collective-permute-start(f32[1,32,512]{2,0,1:T(1,128)S(1)} %get-tuple-element.43), channel_id=1, source_target_pairs={{8,0},{16,8},{24,16},{32,24},{40,32},{48,40},{56,48},{64,56},{72,6... | collective-permute-start | bytes 196616 | tf_op jit(solution)/shard_map/ppermute | solution.py:24
  359.9 10.5 %collective-permute-start.16 = (f32[34,1,512]{2,0,1:T(8,128)S(1)}, f32[34,1,512]{2,0,1:T(8,128)S(1)}, u32[]{:S(2)}, u32[]{:S(2)}) collective-permute-start(f32[34,1,512]{2,0,1:T(8,128)S(1)} %get-tuple-element.32), channel_id=1, source_target_pairs={{0,1},{1,2},{2,3},{3,4},{4,5},{5,6},{6,7},{8,9},{9,10},{10,11},{11... | collective-permute-start | bytes 208904 | tf_op jit(solution)/shard_map/ppermute | solution.py:22
  361.9 8.6 %copy-start.11 = (f32[32,32,511]{2,0,1:T(8,128)S(1)}, f32[32,32,511]{2,0,1:T(8,128)}, u32[]{:S(2)}) copy-start(f32[32,32,511]{2,0,1:T(8,128)} %copy-done.9) | copy-start | bytes 6279172
  361.9 8.6 %copy-start.15 = (f32[32,32,512]{2,1,0:T(8,128)S(1)}, f32[32,32,512]{2,1,0:T(8,128)}, u32[]{:S(2)}) copy-start(f32[32,32,512]{2,1,0:T(8,128)} %param.4) | copy-start | bytes 6291460
  361.9 8.5 %collective-permute-start.17 = (f32[34,1,512]{2,0,1:T(8,128)S(1)}, f32[34,1,512]{2,0,1:T(8,128)S(1)}, u32[]{:S(2)}, u32[]{:S(2)}) collective-permute-start(f32[34,1,512]{2,0,1:T(8,128)S(1)} %get-tuple-element.33), channel_id=1, source_target_pairs={{1,0},{2,1},{3,2},{4,3},{5,4},{6,5},{7,6},{9,8},{10,9},{11,10},{12... | collective-permute-start | bytes 208904 | tf_op jit(solution)/shard_map/ppermute | solution.py:24
  382.7 36.1 %copy-start.21 = (f32[32,32,512]{2,0,1:T(8,128)S(1)}, f32[32,32,512]{2,0,1:T(8,128)}, u32[]{:S(2)}) copy-start(f32[32,32,512]{2,0,1:T(8,128)} %fusion.11) | copy-start | bytes 6291460
  463.8 8.9 %copy-start.19 = (f32[32,32,512]{2,0,1:T(8,128)S(1)}, f32[32,32,512]{2,0,1:T(8,128)}, u32[]{:S(2)}) copy-start(f32[32,32,512]{2,0,1:T(8,128)} %copy-done.18) | copy-start | bytes 6291460
  465.0 113.3 %all-to-all-start = ((f32[1,64,16,256]{3,2,0,1:T(8,128)}), f32[1,64,16,256]{3,2,0,1:T(8,128)}, u32[]{:S(2)}, u32[]{:S(2)}) async-start(f32[1,64,16,256]{3,2,0,1:T(8,128)} %fusion.75), calls=%async_computation | async-start | bytes 2097152 | tf_op jit(solution)/shard_map/all_to_all | solution.py:182
  547.8 3.1 copy-start.25
  554.3 3.4 copy-start.26
  554.3 3.5 copy-start.24
  568.2 2.5 copy-start.27
  568.2 2.5 copy-start.28
  578.3 8.4 %copy-start.5 = (f32[32,32,512]{2,0,1:T(8,128)S(1)}, f32[32,32,512]{2,0,1:T(8,128)}, u32[]{:S(2)}) copy-start(f32[32,32,512]{2,0,1:T(8,128)} %copy-done.4) | copy-start | bytes 6291460
  578.3 66.0 %all-to-all-start.1 = ((f32[4,64,16,256]{3,2,0,1:T(8,128)}), f32[4,64,16,256]{3,2,0,1:T(8,128)}, u32[]{:S(2)}, u32[]{:S(2)}) async-start(f32[4,64,16,256]{3,2,0,1:T(8,128)} %select_bitcast_fusion), calls=%async_computation.1 | async-start | bytes 8388608 | tf_op jit(solution)/shard_map/all_to_all | solution.py:183
  (2 other events, 3.0 us)
where the time goes:
time: 662 us; the launch traced here: 654 us
  local copies, waits for them, and re-layouts  415 us (63%)
  other arithmetic  87.8 us (13%)
  starting transfers between devices  78.7 us (12%)
  waiting for transfers between devices  70.5 us (11%)
    slice x8, local copies, waits for them, and re-layouts, pair_sum_z(): return field[..., 0::2] + field[..., 1::2]  286 us
    all_to_all x1, waiting for transfers between devices, local(): lax.all_to_all(coef_send, 'gx', split_axis=1, concat_axis=1, tiled=True)  52.5 us
    add x3, other arithmetic, smooth_each(): solution = solution + update  44.2 us
    slice x1, local copies, waits for them, and re-layouts, average_faces(): along_z = jnp.sum(split_major(faces[2][..., 0::2]), axis=(1, 3)) * 0.25  36.5 us
    ppermute x8, starting transfers between devices, padded_2(): lax.ppermute(head, axis, [((i + 1) % count, i) for i in range(ends)])  30.3 us
    ppermute x8, starting transfers between devices, padded_2(): lax.ppermute(tail, axis, [(i, (i + 1) % count) for i in range(ends)])  25.6 us
    ppermute x8, waiting for transfers between devices, padded_2(): lax.ppermute(head, axis, [((i + 1) % count, i) for i in range(ends)])  18 us
    slice x4, local copies, waits for them, and re-layouts, shift_lower(): field[..., :-1]  13.4 us
  transfers between devices with their start and end apart: 20, of which 4 were waited for; matrix products, arithmetic and copies ran while one was open for 51% of the time, Pallas kernels for 0%

commit v1 on v0

v1 whole, which is shorter than its diff:
```python
import functools

import jax
import jax.numpy as jnp
from jax import lax
from jax.experimental import pallas as pl
from jax.experimental.pallas import tpu as pltpu
from jax.sharding import PartitionSpec as P

ITERS = 4
CHEB_HIGH = 2.0
CHEB_LOW = 0.25

MESH = pl.DeviceIdType.MESH
LANES = 128
N_GX = 16
Y0 = 8


def chebyshev_steps():
    theta = (CHEB_HIGH + CHEB_LOW) / 2.0
    delta = (CHEB_HIGH - CHEB_LOW) / 2.0
    sigma = theta / delta
    rho = 1.0 / sigma
    steps = []
    for _ in range(ITERS - 1):
        rho_next = 1.0 / (2.0 * sigma - rho)
        steps.append((rho_next * rho, 2.0 * rho_next / delta))
        rho = rho_next
    return theta, steps


def kernel(
    n_gy,
    owner_ref,
    b_hbm,
    alpha_hbm,
    face_hbm,
    sol_hbm,
    cres_hbm,
    ccoef_hbm,
    B,
    AL,
    FX,
    FY,
    FZ,
    FZU,
    INV,
    DG,
    V,
    RES,
    YP,
    YR,
    FYP,
    FYR,
    SB,
    CB,
    T,
    RA,
    RB,
    RC,
    S2,
    box_of,
    load_sem,
    face_send,
    face_recv,
    halo_send,
    halo_recv,
    one_send,
    one_recv,
    one_local,
    two_send,
    two_recv,
    two_local,
    out_sem,
):
    nx, ny = 32, 32
    nl = 4
    gx = lax.axis_index("gx")
    gy = lax.axis_index("gy")
    bx, r = gx // 4, gx % 4
    theta, steps = chebyshev_steps()

    def load(src, dst, which, lt):
        return pltpu.make_async_copy(src, dst, load_sem.at[which, lt])

    loads = []
    for lt in range(nl):
        cols = pl.ds(lt * LANES, LANES)
        loads.append(
            [
                load(face_hbm.at[0, :, :, cols], FX.at[lt, pl.ds(0, nx)], 0, lt),
                load(face_hbm.at[1, :, :, cols], FY.at[lt, :, pl.ds(0, ny)], 1, lt),
                load(face_hbm.at[2, :, :, cols], FZ.at[lt], 2, lt),
                load(alpha_hbm.at[:, :, cols], AL.at[lt], 3, lt),
                load(b_hbm.at[:, :, cols], B.at[lt], 4, lt),
            ]
        )
    for which in range(5):
        for lt in range(nl):
            loads[lt][which].start()

    zero_plane = jnp.zeros((ny, LANES), jnp.float32)
    for lt in range(nl):
        FX[lt, nx] = zero_plane
        FYR[lt] = zero_plane
        for k in range(ITERS):
            V[k, lt, 0, Y0 : Y0 + ny] = zero_plane
            V[k, lt, nx + 1, Y0 : Y0 + ny] = zero_plane
            YR[k, 0, lt] = zero_plane
            YR[k, 1, lt] = zero_plane

    barrier = pltpu.get_barrier_semaphore()

    @pl.loop(1, N_GX)
    def _(d):
        pl.semaphore_signal(
            barrier, inc=1, device_id=(lax.rem(gx + d, N_GX), gy), device_id_type=MESH
        )

    has_up = gy < n_gy - 1
    has_down = gy > 0

    @pl.when(has_down)
    def _():
        pl.semaphore_signal(barrier, inc=1, device_id=(gx, gy - 1), device_id_type=MESH)

    @pl.when(has_up)
    def _():
        pl.semaphore_signal(barrier, inc=1, device_id=(gx, gy + 1), device_id_type=MESH)

    owners = [owner_ref[0, (4 * (b // 4)) * 16 + 4 * (b % 4)] for b in range(16)]
    for o in range(16):
        found = jnp.int32(0)
        for b in range(16):
            found = jnp.where(owners[b] == o, jnp.int32(b), found)
        box_of[o] = found

    sides = jnp.where(has_down, 1, 0) + jnp.where(has_up, 1, 0)
    pl.semaphore_wait(barrier, N_GX - 1 + sides)

    def remote(src, dst, send, recv, to_x, to_y):
        return pltpu.make_async_remote_copy(
            src_ref=src,
            dst_ref=dst,
            send_sem=send,
            recv_sem=recv,
            device_id=(to_x, to_y),
            device_id_type=MESH,
        )

    def guarded(pred, fn):
        @pl.when(pred)
        def _():
            fn()

    x_low, x_high = gx > 0, gx < N_GX - 1

    face_x = remote(
        FX.at[:, pl.ds(0, 1)], FX.at[:, pl.ds(nx, 1)], face_send.at[0], face_recv.at[0], gx - 1, gy
    )
    face_y = remote(FYP, FYR, face_send.at[1], face_recv.at[1], gx, gy - 1)
    for lt in range(nl):
        loads[lt][0].wait()
    guarded(x_low, face_x.start)
    fy_flat = FY.reshape(nl, nx * 40, LANES)
    for lt in range(nl):
        loads[lt][1].wait()
        FYP[lt] = fy_flat[lt, pl.ds(0, nx, stride=40), :]
    guarded(has_down, face_y.start)
    for which in range(2, 5):
        for lt in range(nl):
            loads[lt][which].wait()

    lane = lax.broadcasted_iota(jnp.int32, (8, LANES), 1)
    first_lane, last_lane = lane == 0, lane == LANES - 1
    blank = jnp.zeros((8, LANES), jnp.float32)

    def z_lower(c):
        turned = [pltpu.roll(ci, 1, axis=1) for ci in c]
        return [
            jnp.where(first_lane, turned[i - 1] if i else blank, turned[i]) for i in range(nl)
        ]

    def z_upper(c):
        turned = [pltpu.roll(ci, LANES - 1, axis=1) for ci in c]
        return [
            jnp.where(last_lane, turned[i + 1] if i < nl - 1 else blank, turned[i])
            for i in range(nl)
        ]

    v_flat = V.reshape(ITERS, nl, (nx + 2) * 48, LANES)

    def halo_copies(k):
        rows = pl.ds(Y0, ny)
        down_x = remote(
            V.at[k, :, pl.ds(1, 1), rows],
            V.at[k, :, pl.ds(nx + 1, 1), rows],
            halo_send.at[k, 0],
            halo_recv.at[k, 0],
            gx - 1,
            gy,
        )
        up_x = remote(
            V.at[k, :, pl.ds(nx, 1), rows],
            V.at[k, :, pl.ds(0, 1), rows],
            halo_send.at[k, 1],
            halo_recv.at[k, 1],
            gx + 1,
            gy,
        )
        down_y = remote(YP.at[k, 0], YR.at[k, 1], halo_send.at[k, 2], halo_recv.at[k, 2], gx, gy - 1)
        up_y = remote(YP.at[k, 1], YR.at[k, 0], halo_send.at[k, 3], halo_recv.at[k, 3], gx, gy + 1)
        return down_x, up_x, down_y, up_y

    halos = [halo_copies(k) for k in range(ITERS)]

    def send_y(k):
        for lt in range(nl):
            YP[k, 0, lt] = v_flat[k, lt, pl.ds(48 + Y0, nx, stride=48), :]
            YP[k, 1, lt] = v_flat[k, lt, pl.ds(48 + Y0 + ny - 1, nx, stride=48), :]
        guarded(has_down, halos[k][2].start)
        guarded(has_up, halos[k][3].start)

    def send_x(k):
        guarded(x_low, halos[k][0].start)
        guarded(x_high, halos[k][1].start)

    def wait_halo(k):
        down_x, up_x, down_y, up_y = halos[k]
        guarded(x_low, down_x.wait_send)
        guarded(x_high, down_x.wait_recv)
        guarded(x_high, up_x.wait_send)
        guarded(x_low, up_x.wait_recv)
        guarded(has_down, down_y.wait_send)
        guarded(has_up, down_y.wait_recv)
        guarded(has_up, up_y.wait_send)
        guarded(has_down, up_y.wait_recv)
        for lt in range(nl):
            v_flat[k, lt, pl.ds(48 + Y0 - 1, nx, stride=48), :] = YR[k, 0, lt]
            v_flat[k, lt, pl.ds(48 + Y0 + ny, nx, stride=48), :] = YR[k, 1, lt]

    def in_parts(body):
        def loop(lo, hi, tiles):
            def step(x, carry):
                body(x, tiles)
                return carry

            lax.fori_loop(lo, hi, step, 0)

        return (
            lambda: loop(0, nx, (0, 3)),
            lambda: (body(0, (1, 2)), body(nx - 1, (1, 2))),
            lambda: loop(1, nx - 1, (1, 2)),
        )

    def first(x, tiles):
        for yt in tiles:
            rows = pl.ds(8 * yt, 8)
            fz = [FZ[lt, x, rows, :] for lt in range(nl)]
            fzu = z_upper(fz)
            for lt in range(nl):
                d = AL[lt, x, rows, :] + FX[lt, x, rows, :] + FX[lt, x + 1, rows, :]
                d = d + FY[lt, x, rows, :] + FY[lt, x, pl.ds(8 * yt + 1, 8), :]
                d = d + fz[lt] + fzu[lt]
                inv = 1.0 / d
                FZU[lt, x, rows, :] = fzu[lt]
                DG[lt, x, rows, :] = d
                INV[lt, x, rows, :] = inv
                V[0, lt, x + 1, pl.ds(Y0 + 8 * yt, 8), :] = inv * B[lt, x, rows, :] * (1.0 / theta)

    def gathered(k, x, yt):
        rows = pl.ds(8 * yt, 8)
        y = Y0 + 8 * yt
        c = [V[k, lt, x + 1, pl.ds(y, 8), :] for lt in range(nl)]
        low, high = z_lower(c), z_upper(c)
        t = []
        for lt in range(nl):
            s = B[lt, x, rows, :] + FX[lt, x, rows, :] * V[k, lt, x, pl.ds(y, 8), :]
            s = s + FX[lt, x + 1, rows, :] * V[k, lt, x + 2, pl.ds(y, 8), :]
            s = s + FY[lt, x, rows, :] * V[k, lt, x + 1, pl.ds(y - 1, 8), :]
            s = s + FY[lt, x, pl.ds(8 * yt + 1, 8), :] * V[k, lt, x + 1, pl.ds(y + 1, 8), :]
            s = s + FZ[lt, x, rows, :] * low[lt] + FZU[lt, x, rows, :] * high[lt]
            t.append(s)
        return t, c

    def sweep(k, c1, c2):
        def body(x, tiles):
            for yt in tiles:
                t, c = gathered(k, x, yt)
                rows = pl.ds(8 * yt, 8)
                y = pl.ds(Y0 + 8 * yt, 8)
                for lt in range(nl):
                    new = (1.0 + c1 - c2) * c[lt] + c2 * (INV[lt, x, rows, :] * t[lt])
                    if k > 0:
                        new = new - c1 * V[k - 1, lt, x + 1, y, :]
                    V[k + 1, lt, x + 1, y, :] = new

        return body

    row_i = lax.broadcasted_iota(jnp.int32, (LANES, LANES), 0)
    col_i = lax.broadcasted_iota(jnp.int32, (LANES, LANES), 1)
    groups = [(lane // 16) // d % 2 == 1 for d in (4, 2, 1)]

    def restrict(f, pairs, weight, even_only):
        def gather(X, carry):
            for lt in range(nl):
                SB[lt, pl.ds(pl.multiple_of(X * 16, 16), 16), :] = pairs(lt, X)
            return carry

        lax.fori_loop(0, 16, gather, 0)
        for half in range(2):
            total = None
            for side in range(2):
                hit = row_i // 2 + 64 * side == col_i
                if even_only:
                    hit = hit & (row_i % 2 == 0)
                pick = jnp.where(hit, weight, 0.0).astype(jnp.float32)
                part = jnp.dot(
                    SB[2 * half + side],
                    pick,
                    precision=lax.Precision.HIGHEST,
                    preferred_element_type=jnp.float32,
                )
                total = part if total is None else total + part
            CB[half] = total.reshape(16, 16, LANES)

        def turn(i, carry):
            half, yt, xt = i // 4, i // 2 % 2, i % 2
            rows = pl.ds(pl.multiple_of(yt * 8, 8), 8)
            a = [CB[half, xt * 8 + j, rows, :] for j in range(8)]
            for d, odd in zip((4, 2, 1), groups):
                b = list(a)
                for j in range(8):
                    if j & d == 0:
                        lo, hi = a[j], a[j + d]
                        b[j] = jnp.where(odd, pltpu.roll(hi, 16 * d, axis=1), lo)
                        b[j + d] = jnp.where(odd, hi, pltpu.roll(lo, LANES - 16 * d, axis=1))
                a = b
            for j in range(8):
                T[f, yt * 2 + xt, half * 2 + j // 4, j % 4] = a[j]
            return carry

        lax.fori_loop(0, 8, turn, 0)

    def strided(ref, lt, x, start):
        return ref[lt, x, pl.ds(start, 16, stride=2), :]

    def four(ref):
        return lambda lt, X: (
            strided(ref, lt, 2 * X, 0)
            + strided(ref, lt, 2 * X, 1)
            + strided(ref, lt, 2 * X + 1, 0)
            + strided(ref, lt, 2 * X + 1, 1)
        )

    spread = (RA, RB, RC)

    def stage_one(f):
        copies = []
        for j in range(1, 4):
            q = lax.rem(bx + j, 4)
            copies.append(
                remote(
                    T.at[f, q],
                    spread[f // 2].at[f % 2, pl.ds(bx * 4, 4)],
                    one_send.at[f, j],
                    one_recv.at[f, j],
                    q * 4 + r,
                    gy,
                )
            )
        own = pltpu.make_async_copy(T.at[f, bx], spread[f // 2].at[f % 2, pl.ds(bx * 4, 4)], one_local.at[f])
        return copies, own

    first_stage = [stage_one(f) for f in range(5)]

    def start_one(f):
        copies, own = first_stage[f]
        for c in copies:
            c.start()
        own.start()

    def wait_one(f):
        copies, own = first_stage[f]
        for c in copies:
            c.wait()
        own.wait()

    yt, xt = bx // 2, bx % 2
    out_rows = pl.ds(pl.multiple_of(r * 4, 4), 4)
    out_y = pl.ds(pl.multiple_of(yt * 8, 8), 8)
    out_cols = pl.ds(pl.multiple_of(xt * LANES, LANES), LANES)
    group_fields = ((0, 2), (2, 4), (4, 5))

    def landing(g):
        lo, hi = group_fields[g]
        if g == 2:
            return cres_hbm.at[:, out_rows, out_y, out_cols]
        return ccoef_hbm.at[pl.ds(lo, hi - lo), out_rows, out_y, out_cols]

    def two_copy(g, d):
        lo, hi = group_fields[g]
        o = lax.rem(gx + d, N_GX)
        return remote(
            S2.at[o, pl.ds(lo, hi - lo)], landing(g), two_send.at[g, d], two_recv.at[g, d], o, gy
        )

    def two_own(g):
        lo, hi = group_fields[g]
        return pltpu.make_async_copy(S2.at[gx, pl.ds(lo, hi - lo)], landing(g), two_local.at[g])

    def start_two(g):
        lo, hi = group_fields[g]

        def pack(o, carry):
            box = box_of[o]
            for f in range(lo, hi):
                S2[o, f] = spread[g][f - lo, box]
            return carry

        lax.fori_loop(0, N_GX, pack, 0)

        @pl.loop(1, N_GX)
        def _(d):
            two_copy(g, d).start()

        two_own(g).start()

    def wait_two(g):
        @pl.loop(1, N_GX)
        def _(d):
            two_copy(g, d).wait()

        two_own(g).wait()

    guarded(x_high, face_x.wait_recv)
    guarded(x_low, face_x.wait_send)
    guarded(has_up, face_y.wait_recv)
    guarded(has_down, face_y.wait_send)
    for lt in range(nl):
        fy_flat[lt, pl.ds(ny, nx, stride=40), :] = FYR[lt]

    def all_parts(k, body):
        y_part, x_part, inner = in_parts(body)
        y_part()
        send_y(k)
        x_part()
        send_x(k)
        inner()

    all_parts(0, first)
    restrict(0, four(AL), 0.125, False)
    start_one(0)
    restrict(
        1, lambda lt, X: strided(FX, lt, 2 * X, 0) + strided(FX, lt, 2 * X, 1), 0.25, False
    )
    start_one(1)
    wait_halo(0)
    all_parts(1, sweep(0, *steps[0]))
    restrict(
        2, lambda lt, X: strided(FY, lt, 2 * X, 0) + strided(FY, lt, 2 * X + 1, 0), 0.25, False
    )
    start_one(2)
    restrict(3, four(FZ), 0.25, True)
    start_one(3)
    wait_halo(1)
    all_parts(2, sweep(1, *steps[1]))
    wait_one(0)
    wait_one(1)
    start_two(0)
    wait_halo(2)
    all_parts(3, sweep(2, *steps[2]))
    outs = [
        pltpu.make_async_copy(
            V.at[3, lt, pl.ds(1, nx), pl.ds(Y0, ny)],
            sol_hbm.at[:, :, pl.ds(lt * LANES, LANES)],
            out_sem.at[lt],
        )
        for lt in range(nl)
    ]
    for o in outs:
        o.start()
    wait_one(2)
    wait_one(3)
    start_two(1)
    wait_halo(3)

    def last(X, carry):
        for yt_ in range(4):
            rows = pl.ds(8 * yt_, 8)
            acc = None
            for a in range(2):
                x = 2 * X + a
                t, c = gathered(3, x, yt_)
                res = [t[lt] - DG[lt, x, rows, :] * c[lt] for lt in range(nl)]
                acc = res if acc is None else [p + q for p, q in zip(acc, res)]
            for lt in range(nl):
                RES[lt, X, rows, :] = acc[lt]
        return carry

    lax.fori_loop(0, 16, last, 0)
    restrict(4, lambda lt, X: strided(RES, lt, X, 0) + strided(RES, lt, X, 1), 0.125, False)
    start_one(4)
    wait_one(4)
    start_two(2)
    for o in outs:
        o.wait()
    for g in range(3):
        wait_two(g)


def local(n_gy, right_side, alpha_coef, face_coef, owner_map):
    f32 = jnp.float32
    vmem = pltpu.VMEM
    dma = pltpu.SemaphoreType.DMA
    hbm = pl.BlockSpec(memory_space=pl.ANY)
    cells = vmem((4, 32, 32, LANES), f32)
    sol, cres, ccoef = pl.pallas_call(
        functools.partial(kernel, n_gy),
        out_shape=(
            jax.ShapeDtypeStruct((32, 32, 512), f32),
            jax.ShapeDtypeStruct((1, 16, 16, 256), f32),
            jax.ShapeDtypeStruct((4, 16, 16, 256), f32),
        ),
        in_specs=[pl.BlockSpec(memory_space=pltpu.SMEM), hbm, hbm, hbm],
        out_specs=(hbm, hbm, hbm),
        scratch_shapes=[
            cells,
            cells,
            vmem((4, 33, 32, LANES), f32),
            vmem((4, 32, 40, LANES), f32),
            cells,
            cells,
            cells,
            cells,
            vmem((ITERS, 4, 34, 48, LANES), f32),
            vmem((4, 16, 32, LANES), f32),
            vmem((ITERS, 2, 4, 32, LANES), f32),
            vmem((ITERS, 2, 4, 32, LANES), f32),
            vmem((4, 32, LANES), f32),
            vmem((4, 32, LANES), f32),
            vmem((4, 256, LANES), f32),
            vmem((2, 16, 16, LANES), f32),
            vmem((5, 4, 4, 4, 8, LANES), f32),
            vmem((2, 16, 4, 8, LANES), f32),
            vmem((2, 16, 4, 8, LANES), f32),
            vmem((1, 16, 4, 8, LANES), f32),
            vmem((16, 5, 4, 8, LANES), f32),
            pltpu.SMEM((16,), jnp.int32),
            dma((5, 4)),
            dma((2,)),
            dma((2,)),
            dma((ITERS, 4)),
            dma((ITERS, 4)),
            dma((5, 4)),
            dma((5, 4)),
            dma((5,)),
            dma((3, 16)),
            dma((3, 16)),
            dma((3,)),
            dma((4,)),
        ],
        compiler_params=pltpu.CompilerParams(
            collective_id=0, has_side_effects=True, vmem_limit_bytes=56 << 20
        ),
        name="smooth_and_restrict",
    )(owner_map, right_side, alpha_coef, face_coef)
    return sol, cres[0], ccoef


def solution(mesh):
    return jax.shard_map(
        functools.partial(local, mesh.shape["gy"]),
        mesh=mesh,
        in_specs=(
            P("gx", "gy", None),
            P("gx", "gy", None),
            P(None, "gx", "gy", None),
            P("gy", None),
        ),
        out_specs=(P("gx", "gy", None), P("gx", "gy", None), P(None, "gx", "gy", None)),
        check_vma=False,
    )
```

time: 662 us -> 79.1 us (0.12)
  the two profiles are of different devices: /device:TPU:29 before, /device:TPU:9 now
where the time goes in v1:
time: 79.1 us; the launch traced here: 79 us
  Pallas kernels  73.3 us (93%)
  local copies, waits for them, and re-layouts  4.97 us (6%)
    pallas_call x1, Pallas kernels, local(): pl.pallas_call(functools.partial(kernel, n_gy), out_shape=(jax.ShapeDtype...  73.3 us
    unnamed x7, local copies, waits for them, and re-layouts  4.97 us

profile of v1, /device:TPU:9, one launch (start us, length us, event | category | flops | bytes accessed | tf_op | source)
XLA Modules:
  0.0 79.0 jit_solution(3972296747194035847)
XLA Ops:
  0.6 73.3 %smooth_and_restrict.1 = (f32[32,32,512]{2,1,0:T(8,128)}, f32[1,16,16,256]{3,2,1,0:T(8,128)}, f32[4,16,16,256]{3,2,1,0:T(8,128)}) custom-call(s32[1,256]{1,0:T(1,128)} %owner_ref.1, f32[32,32,512]{2,1,0:T(8,128)} %b_hbm.1, f32[32,32,512]{2,1,0:T(8,128)} %alpha_hbm.1, f32[3,32,32,512]{3,2,1,0:T(8,128)} %face_hbm.1), custom_call_target="tpu_custom_call" | custom-call | tf_op jit(solution)/shard_map/smooth_and_restrict/pallas_call | solution.py:519
  74.0 0.0 copy-start.1
  74.0 0.0 copy-start
  74.0 3.3 %copy.10 = f32[32,32,512]{2,1,0:T(8,128)} copy(f32[32,32,512]{2,1,0:T(8,128)} %get-tuple-element.12) | data formatting | bytes 4194304
  77.3 0.0 copy-done.1
  77.3 0.7 copy.11
  78.0 0.0 copy-done
  78.0 1.0 %copy.12 = f32[4,16,16,256]{3,2,1,0:T(8,128)} copy(f32[4,16,16,256]{3,2,1,0:T(8,128)S(1)} %copy-done) | data formatting | bytes 2097152
Async XLA Ops:
  74.0 3.3 %copy-start.1 = (f32[1,16,16,256]{3,2,1,0:T(8,128)S(1)}, f32[1,16,16,256]{3,2,1,0:T(8,128)}, u32[]{:S(2)}) copy-start(f32[1,16,16,256]{3,2,1,0:T(8,128)} %get-tuple-element.7) | copy-start | bytes 786436
  74.0 4.0 %copy-start = (f32[4,16,16,256]{3,2,1,0:T(8,128)S(1)}, f32[4,16,16,256]{3,2,1,0:T(8,128)}, u32[]{:S(2)}) copy-start(f32[4,16,16,256]{3,2,1,0:T(8,128)} %get-tuple-element.14) | copy-start | bytes 3145732

commit v2 on v1

--- a/solution.py
+++ b/solution.py
@@ -36,9 +36,9 @@
     b_hbm,
     alpha_hbm,
     face_hbm,
-    sol_hbm,
-    cres_hbm,
-    ccoef_hbm,
+    sol_ref,
+    cres_ref,
+    ccoef_ref,
     B,
     AL,
     FX,
@@ -59,6 +59,8 @@
     RA,
     RB,
     RC,
+    RD,
+    RE,
     S2,
     box_of,
     load_sem,
@@ -72,7 +74,6 @@
     two_send,
     two_recv,
     two_local,
-    out_sem,
 ):
     nx, ny = 32, 32
     nl = 4
@@ -160,17 +161,18 @@
         FX.at[:, pl.ds(0, 1)], FX.at[:, pl.ds(nx, 1)], face_send.at[0], face_recv.at[0], gx - 1, gy
     )
     face_y = remote(FYP, FYR, face_send.at[1], face_recv.at[1], gx, gy - 1)
+    fy_flat = FY.reshape(nl, nx * 40, LANES)
+
+    def wait_load(which):
+        for lt in range(nl):
+            loads[lt][which].wait()
+
+    wait_load(0)
+    guarded(x_low, face_x.start)
+    wait_load(1)
     for lt in range(nl):
-        loads[lt][0].wait()
-    guarded(x_low, face_x.start)
-    fy_flat = FY.reshape(nl, nx * 40, LANES)
-    for lt in range(nl):
-        loads[lt][1].wait()
         FYP[lt] = fy_flat[lt, pl.ds(0, nx, stride=40), :]
     guarded(has_down, face_y.start)
-    for which in range(2, 5):
-        for lt in range(nl):
-            loads[lt][which].wait()
 
     lane = lax.broadcasted_iota(jnp.int32, (8, LANES), 1)
     first_lane, last_lane = lane == 0, lane == LANES - 1
@@ -216,9 +218,6 @@
     halos = [halo_copies(k) for k in range(ITERS)]
 
     def send_y(k):
-        for lt in range(nl):
-            YP[k, 0, lt] = v_flat[k, lt, pl.ds(48 + Y0, nx, stride=48), :]
-            YP[k, 1, lt] = v_flat[k, lt, pl.ds(48 + Y0 + ny - 1, nx, stride=48), :]
         guarded(has_down, halos[k][2].start)
         guarded(has_up, halos[k][3].start)
 
@@ -240,19 +239,12 @@
             v_flat[k, lt, pl.ds(48 + Y0 - 1, nx, stride=48), :] = YR[k, 0, lt]
             v_flat[k, lt, pl.ds(48 + Y0 + ny, nx, stride=48), :] = YR[k, 1, lt]
 
-    def in_parts(body):
-        def loop(lo, hi, tiles):
-            def step(x, carry):
-                body(x, tiles)
-                return carry
-
-            lax.fori_loop(lo, hi, step, 0)
-
-        return (
-            lambda: loop(0, nx, (0, 3)),
-            lambda: (body(0, (1, 2)), body(nx - 1, (1, 2))),
-            lambda: loop(1, nx - 1, (1, 2)),
-        )
+    def planes(body, lo, hi, tiles, unroll):
+        def step(x, carry):
+            body(x, tiles)
+            return carry
+
+        lax.fori_loop(lo, hi, step, 0, unroll=unroll)
 
     def first(x, tiles):
         for yt in tiles:
@@ -295,53 +287,82 @@
                     if k > 0:
                         new = new - c1 * V[k - 1, lt, x + 1, y, :]
                     V[k + 1, lt, x + 1, y, :] = new
+                    if k == ITERS - 2:
+                        sol_ref[x, rows, lt * LANES : (lt + 1) * LANES] = new
 
         return body
+
+    flat = {n: r.reshape(nl, nx * ny, LANES) for n, r in (("b", B), ("z", FZ), ("zu", FZU), ("inv", INV))}
+    fx_flat = FX.reshape(nl, (nx + 1) * ny, LANES)
+
+    def edge_rows(k, c1, c2):
+        for side, y in ((0, 0), (1, ny - 1)):
+            for j in range(nx // 8):
+
+                def v_row(kk, lt, dx, dy):
+                    return v_flat[
+                        kk, lt, pl.ds((1 + 8 * j + dx) * 48 + Y0 + y + dy, 8, stride=48), :
+                    ]
+
+                def row(ref, lt, dx=0):
+                    return ref[lt, pl.ds((8 * j + dx) * ny + y, 8, stride=ny), :]
+
+                c = [v_row(k, lt, 0, 0) for lt in range(nl)]
+                low, high = z_lower(c), z_upper(c)
+                for lt in range(nl):
+                    t = row(flat["b"], lt) + row(fx_flat, lt) * v_row(k, lt, -1, 0)
+                    t = t + row(fx_flat, lt, 1) * v_row(k, lt, 1, 0)
+                    at = 8 * j * 40 + y
+                    t = t + fy_flat[lt, pl.ds(at, 8, stride=40), :] * v_row(k, lt, 0, -1)
+                    t = t + fy_flat[lt, pl.ds(at + 1, 8, stride=40), :] * v_row(k, lt, 0, 1)
+                    t = t + row(flat["z"], lt) * low[lt] + row(flat["zu"], lt) * high[lt]
+                    new = (1.0 + c1 - c2) * c[lt] + c2 * (row(flat["inv"], lt) * t)
+                    if k > 0:
+                        new = new - c1 * v_row(k - 1, lt, 0, 0)
+                    YP[k + 1, side, lt, 8 * j : 8 * j + 8] = new
 
     row_i = lax.broadcasted_iota(jnp.int32, (LANES, LANES), 0)
     col_i = lax.broadcasted_iota(jnp.int32, (LANES, LANES), 1)
     groups = [(lane // 16) // d % 2 == 1 for d in (4, 2, 1)]
 
-    def restrict(f, pairs, weight, even_only):
+    def restrict(f, pairs, weight, even_only, first_x=0, last_x=16):
         def gather(X, carry):
             for lt in range(nl):
                 SB[lt, pl.ds(pl.multiple_of(X * 16, 16), 16), :] = pairs(lt, X)
             return carry
 
-        lax.fori_loop(0, 16, gather, 0)
+        lax.fori_loop(first_x, last_x, gather, 0, unroll=4)
         for half in range(2):
             total = None
             for side in range(2):
                 hit = row_i // 2 + 64 * side == col_i
                 if even_only:
                     hit = hit & (row_i % 2 == 0)
-                pick = jnp.where(hit, weight, 0.0).astype(jnp.float32)
-                part = jnp.dot(
-                    SB[2 * half + side],
-                    pick,
-                    precision=lax.Precision.HIGHEST,
-                    preferred_element_type=jnp.float32,
-                )
-                total = part if total is None else total + part
-            CB[half] = total.reshape(16, 16, LANES)
-
-        def turn(i, carry):
-            half, yt, xt = i // 4, i // 2 % 2, i % 2
-            rows = pl.ds(pl.multiple_of(yt * 8, 8), 8)
-            a = [CB[half, xt * 8 + j, rows, :] for j in range(8)]
-            for d, odd in zip((4, 2, 1), groups):
-                b = list(a)
-                for j in range(8):
-                    if j & d == 0:
-                        lo, hi = a[j], a[j + d]
-                        b[j] = jnp.where(odd, pltpu.roll(hi, 16 * d, axis=1), lo)
-                        b[j + d] = jnp.where(odd, hi, pltpu.roll(lo, LANES - 16 * d, axis=1))
-                a = b
-            for j in range(8):
-                T[f, yt * 2 + xt, half * 2 + j // 4, j % 4] = a[j]
-            return carry
-
-        lax.fori_loop(0, 8, turn, 0)
+                pick = jnp.where(hit, weight, 0.0).astype(jnp.float32).astype(jnp.bfloat16)
+                rest = SB[2 * half + side, first_x * 16 : last_x * 16]
+                for _ in range(3):
+                    piece = rest.astype(jnp.bfloat16)
+                    rest = rest - piece.astype(jnp.float32)
+                    part = jnp.dot(piece, pick, preferred_element_type=jnp.float32)
+                    total = part if total is None else total + part
+            CB[half, first_x:last_x] = total.reshape(last_x - first_x, 16, LANES)
+
+        for half in range(2):
+            for yt in range(2):
+                for xt in range(first_x // 8, last_x // 8):
+                    a = [CB[half, xt * 8 + j, 8 * yt : 8 * yt + 8, :] for j in range(8)]
+                    for d, odd in zip((4, 2, 1), groups):
+                        b = list(a)
+                        for j in range(8):
+                            if j & d == 0:
+                                lo, hi = a[j], a[j + d]
+                                b[j] = jnp.where(odd, pltpu.roll(hi, 16 * d, axis=1), lo)
+                                b[j + d] = jnp.where(
+                                    odd, hi, pltpu.roll(lo, LANES - 16 * d, axis=1)
+                                )
+                        a = b
+                    for j in range(8):
+                        T[f, yt * 2 + xt, half * 2 + j // 4, j % 4] = a[j]
 
     def strided(ref, lt, x, start):
         return ref[lt, x, pl.ds(start, 16, stride=2), :]
@@ -354,7 +375,7 @@
             + strided(ref, lt, 2 * X + 1, 1)
         )
 
-    spread = (RA, RB, RC)
+    spread = (RA, RB, RC, RD, RE)
 
     def stage_one(f):
         copies = []
@@ -363,17 +384,17 @@
             copies.append(
                 remote(
                     T.at[f, q],
-                    spread[f // 2].at[f % 2, pl.ds(bx * 4, 4)],
+                    spread[f].at[pl.ds(bx * 4, 4)],
                     one_send.at[f, j],
                     one_recv.at[f, j],
                     q * 4 + r,
                     gy,
                 )
             )
-        own = pltpu.make_async_copy(T.at[f, bx], spread[f // 2].at[f % 2, pl.ds(bx * 4, 4)], one_local.at[f])
+        own = pltpu.make_async_copy(T.at[f, bx], spread[f].at[pl.ds(bx * 4, 4)], one_local.at[f])
         return copies, own
 
-    first_stage = [stage_one(f) for f in range(5)]
+    first_stage = [stage_one(f) for f in range(4)]
 
     def start_one(f):
         copies, own = first_stage[f]
@@ -387,107 +408,123 @@
             c.wait()
         own.wait()
 
+    mine = RE.at[pl.ds(bx * 4, 4)]
+
+    def residual_quarter(q, source):
+        return remote(
+            T.at[4, q], mine, one_send.at[4, q], one_recv.at[4, source], q * 4 + r, gy
+        )
+
+    own_quarter = pltpu.make_async_copy(T.at[4, bx], mine, one_local.at[4])
+
+    def start_residual(q):
+        guarded(bx != q, residual_quarter(q, bx).start)
+        guarded(bx == q, own_quarter.start)
+
+    def wait_residual():
+        for q in range(4):
+            guarded(bx != q, residual_quarter(q, bx).wait_send)
+        for source in range(4):
+            guarded(bx != source, residual_quarter(0, source).wait_recv)
+        own_quarter.wait()
+
     yt, xt = bx // 2, bx % 2
     out_rows = pl.ds(pl.multiple_of(r * 4, 4), 4)
     out_y = pl.ds(pl.multiple_of(yt * 8, 8), 8)
     out_cols = pl.ds(pl.multiple_of(xt * LANES, LANES), LANES)
-    group_fields = ((0, 2), (2, 4), (4, 5))
-
-    def landing(g):
-        lo, hi = group_fields[g]
-        if g == 2:
-            return cres_hbm.at[:, out_rows, out_y, out_cols]
-        return ccoef_hbm.at[pl.ds(lo, hi - lo), out_rows, out_y, out_cols]
-
-    def two_copy(g, d):
-        lo, hi = group_fields[g]
+
+    def landing(f):
+        if f == 4:
+            return cres_ref.at[out_rows, out_y, out_cols]
+        return ccoef_ref.at[f, out_rows, out_y, out_cols]
+
+    def two_copy(f, d):
         o = lax.rem(gx + d, N_GX)
-        return remote(
-            S2.at[o, pl.ds(lo, hi - lo)], landing(g), two_send.at[g, d], two_recv.at[g, d], o, gy
-        )
-
-    def two_own(g):
-        lo, hi = group_fields[g]
-        return pltpu.make_async_copy(S2.at[gx, pl.ds(lo, hi - lo)], landing(g), two_local.at[g])
-
-    def start_two(g):
-        lo, hi = group_fields[g]
-
+        return remote(S2.at[f, o], landing(f), two_send.at[f, d], two_recv.at[f, d], o, gy)
+
+    def two_own(f):
+        return pltpu.make_async_copy(S2.at[f, gx], landing(f), two_local.at[f])
+
+    def start_two(f):
         def pack(o, carry):
-            box = box_of[o]
-            for f in range(lo, hi):
-                S2[o, f] = spread[g][f - lo, box]
+            S2[f, o] = spread[f][box_of[o]]
             return carry
 
-        lax.fori_loop(0, N_GX, pack, 0)
+        lax.fori_loop(0, N_GX, pack, 0, unroll=4)
 
         @pl.loop(1, N_GX)
         def _(d):
-            two_copy(g, d).start()
-
-        two_own(g).start()
-
-    def wait_two(g):
+            two_copy(f, d).start()
+
+        two_own(f).start()
+
+    def wait_two(f):
         @pl.loop(1, N_GX)
         def _(d):
-            two_copy(g, d).wait()
-
-        two_own(g).wait()
-
+            two_copy(f, d).wait()
+
+        two_own(f).wait()
+
+    def advance(k):
+        body = sweep(k, *steps[k])
+        body(0, (0, 1, 2, 3))
+        body(nx - 1, (0, 1, 2, 3))
+        send_x(k + 1)
+        edge_rows(k, *steps[k])
+        send_y(k + 1)
+        planes(body, 1, nx - 1, (0, 1, 2, 3), 5)
+
+    def restrict_y():
+        def pairs(lt, X):
+            return strided(FY, lt, 2 * X, 0) + strided(FY, lt, 2 * X + 1, 0)
+
+        restrict(2, pairs, 0.25, False)
+
+    def restrict_x():
+        def pairs(lt, X):
+            return strided(FX, lt, 2 * X, 0) + strided(FX, lt, 2 * X, 1)
+
+        restrict(1, pairs, 0.25, False)
+
+    restrict_y()
+    start_one(2)
+    for which in (2, 3, 4):
+        wait_load(which)
+    planes(first, 0, nx - 1, (0, 1, 2), 2)
     guarded(x_high, face_x.wait_recv)
     guarded(x_low, face_x.wait_send)
     guarded(has_up, face_y.wait_recv)
     guarded(has_down, face_y.wait_send)
     for lt in range(nl):
         fy_flat[lt, pl.ds(ny, nx, stride=40), :] = FYR[lt]
-
-    def all_parts(k, body):
-        y_part, x_part, inner = in_parts(body)
-        y_part()
-        send_y(k)
-        x_part()
-        send_x(k)
-        inner()
-
-    all_parts(0, first)
+    first(nx - 1, (0, 1, 2))
+    planes(first, 0, nx, (3,), 4)
+    send_x(0)
+    for lt in range(nl):
+        YP[0, 0, lt] = v_flat[0, lt, pl.ds(48 + Y0, nx, stride=48), :]
+        YP[0, 1, lt] = v_flat[0, lt, pl.ds(48 + Y0 + ny - 1, nx, stride=48), :]
+    send_y(0)
+    restrict(3, four(FZ), 0.25, True)
+    start_one(3)
     restrict(0, four(AL), 0.125, False)
     start_one(0)
-    restrict(
-        1, lambda lt, X: strided(FX, lt, 2 * X, 0) + strided(FX, lt, 2 * X, 1), 0.25, False
-    )
+    wait_halo(0)
+    advance(0)
+    restrict_x()
     start_one(1)
-    wait_halo(0)
-    all_parts(1, sweep(0, *steps[0]))
-    restrict(
-        2, lambda lt, X: strided(FY, lt, 2 * X, 0) + strided(FY, lt, 2 * X + 1, 0), 0.25, False
-    )
-    start_one(2)
-    restrict(3, four(FZ), 0.25, True)
-    start_one(3)
+    wait_one(2)
+    start_two(2)
     wait_halo(1)
-    all_parts(2, sweep(1, *steps[1]))
+    advance(1)
+    wait_one(3)
+    start_two(3)
+    wait_halo(2)
+    advance(2)
     wait_one(0)
-    wait_one(1)
     start_two(0)
-    wait_halo(2)
-    all_parts(3, sweep(2, *steps[2]))
-    outs = [
-        pltpu.make_async_copy(
-            V.at[3, lt, pl.ds(1, nx), pl.ds(Y0, ny)],
-            sol_hbm.at[:, :, pl.ds(lt * LANES, LANES)],
-            out_sem.at[lt],
-        )
-        for lt in range(nl)
-    ]
-    for o in outs:
-        o.start()
-    wait_one(2)
-    wait_one(3)
-    start_two(1)
-    wait_halo(3)
-
-    def last(X, carry):
-        for yt_ in range(4):
+
+    def last(X, tiles):
+        for yt_ in tiles:
             rows = pl.ds(8 * yt_, 8)
             acc = None
             for a in range(2):
@@ -497,17 +534,31 @@
                 acc = res if acc is None else [p + q for p, q in zip(acc, res)]
             for lt in range(nl):
                 RES[lt, X, rows, :] = acc[lt]
-        return carry
-
-    lax.fori_loop(0, 16, last, 0)
-    restrict(4, lambda lt, X: strided(RES, lt, X, 0) + strided(RES, lt, X, 1), 0.125, False)
-    start_one(4)
-    wait_one(4)
-    start_two(2)
-    for o in outs:
-        o.wait()
-    for g in range(3):
-        wait_two(g)
+
+    def restrict_residual(lo, hi):
+        def pairs(lt, X):
+            return strided(RES, lt, X, 0) + strided(RES, lt, X, 1)
+
+        restrict(4, pairs, 0.125, False, lo, hi)
+
+    planes(last, 1, 15, (1, 2), 2)
+    wait_halo(3)
+    last(0, (0, 1, 2, 3))
+    planes(last, 1, 8, (0, 3), 7)
+    restrict_residual(0, 8)
+    start_residual(0)
+    start_residual(2)
+    planes(last, 8, 15, (0, 3), 7)
+    last(15, (0, 1, 2, 3))
+    restrict_residual(8, 16)
+    start_residual(1)
+    start_residual(3)
+    wait_one(1)
+    start_two(1)
+    wait_residual()
+    start_two(4)
+    for f in range(5):
+        wait_two(f)
 
 
 def local(n_gy, right_side, alpha_coef, face_coef, owner_map):
@@ -516,15 +567,16 @@
     dma = pltpu.SemaphoreType.DMA
     hbm = pl.BlockSpec(memory_space=pl.ANY)
     cells = vmem((4, 32, 32, LANES), f32)
+    on_chip = pl.BlockSpec(memory_space=pltpu.VMEM)
     sol, cres, ccoef = pl.pallas_call(
         functools.partial(kernel, n_gy),
         out_shape=(
-            jax.ShapeDtypeStruct((32, 32, 512), f32),
-            jax.ShapeDtypeStruct((1, 16, 16, 256), f32),
-            jax.ShapeDtypeStruct((4, 16, 16, 256), f32),
+            vmem((32, 32, 512), f32),
+            vmem((16, 16, 256), f32),
+            vmem((4, 16, 16, 256), f32),
         ),
         in_specs=[pl.BlockSpec(memory_space=pltpu.SMEM), hbm, hbm, hbm],
-        out_specs=(hbm, hbm, hbm),
+        out_specs=(on_chip, on_chip, on_chip),
         scratch_shapes=[
             cells,
             cells,
@@ -543,10 +595,8 @@
             vmem((4, 256, LANES), f32),
             vmem((2, 16, 16, LANES), f32),
             vmem((5, 4, 4, 4, 8, LANES), f32),
-            vmem((2, 16, 4, 8, LANES), f32),
-            vmem((2, 16, 4, 8, LANES), f32),
-            vmem((1, 16, 4, 8, LANES), f32),
-            vmem((16, 5, 4, 8, LANES), f32),
+            *[vmem((16, 4, 8, LANES), f32)] * 5,
+            vmem((5, 16, 4, 8, LANES), f32),
             pltpu.SMEM((16,), jnp.int32),
             dma((5, 4)),
             dma((2,)),
@@ -556,17 +606,16 @@
             dma((5, 4)),
             dma((5, 4)),
             dma((5,)),
-            dma((3, 16)),
-            dma((3, 16)),
-            dma((3,)),
-            dma((4,)),
+            dma((5, 16)),
+            dma((5, 16)),
+            dma((5,)),
         ],
         compiler_params=pltpu.CompilerParams(
-            collective_id=0, has_side_effects=True, vmem_limit_bytes=56 << 20
+            collective_id=0, has_side_effects=True, vmem_limit_bytes=60 << 20
         ),
         name="smooth_and_restrict",
     )(owner_map, right_side, alpha_coef, face_coef)
-    return sol, cres[0], ccoef
+    return sol, cres, ccoef
 
 
 def solution(mesh):

time: 79.1 us -> 59 us (0.75)
  Pallas kernels: 73.3 us -> 55.1 us
  local copies, waits for them, and re-layouts: 4.97 us -> 2.99 us
    pallas_call x1, Pallas kernels: 73.3 us -> 55.1 us  [local(): pl.pallas_call(functools.partial(kernel, n_gy), out_shape=(vmem((32, 32,...]
    unnamed x7 -> x3, local copies, waits for them, and re-layouts: 4.97 us -> 2.99 us
where the time goes in v2:
time: 59 us; the launch traced here: 58.8 us
  Pallas kernels  55.1 us (93%)
  local copies, waits for them, and re-layouts  2.99 us (5%)
  between operations  0.64 us (1%)
    pallas_call x1, Pallas kernels, local(): pl.pallas_call(functools.partial(kernel, n_gy), out_shape=(vmem((32, 32,...  55.1 us
    unnamed x3, local copies, waits for them, and re-layouts  2.99 us

profile of v2, /device:TPU:9, one launch (start us, length us, event | category | flops | bytes accessed | tf_op | source)
XLA Modules:
  0.0 58.8 jit_solution(4104497574302549072)
XLA Ops:
  0.6 55.1 %smooth_and_restrict.1 = (f32[32,32,512]{2,1,0:T(8,128)S(1)}, f32[16,16,256]{2,1,0:T(8,128)S(1)}, f32[4,16,16,256]{3,2,1,0:T(8,128)S(1)}) custom-call(s32[1,256]{1,0:T(1,128)} %owner_ref.1, f32[32,32,512]{2,1,0:T(8,128)} %b_hbm.1, f32[32,32,512]{2,1,0:T(8,128)} %alpha_hbm.1, f32[3,32,32,512]{3,2,1,0:T(8,128)} %face_hbm.1), custom_call_target="tpu_custom_call" | custom-call | tf_op jit(solution)/shard_map/smooth_and_restrict/pallas_call | solution.py:571
  55.8 1.3 %copy.10 = f32[32,32,512]{2,1,0:T(8,128)} copy(f32[32,32,512]{2,1,0:T(8,128)S(1)} %get-tuple-element.3) | data formatting | bytes 4194304
  57.1 0.7 %copy.11 = f32[16,16,256]{2,1,0:T(8,128)} copy(f32[16,16,256]{2,1,0:T(8,128)S(1)} %get-tuple-element.4) | data formatting | bytes 524288
  57.8 1.0 %copy.12 = f32[4,16,16,256]{3,2,1,0:T(8,128)} copy(f32[4,16,16,256]{3,2,1,0:T(8,128)S(1)} %get-tuple-element.5) | data formatting | bytes 2097152

commit v3 on v2

--- a/solution.py
+++ b/solution.py
@@ -49,10 +49,12 @@
     DG,
     V,
     RES,
-    YP,
+    YX,
     YR,
+    EC,
     FYP,
     FYR,
+    FXR,
     SB,
     CB,
     T,
@@ -104,6 +106,7 @@
     zero_plane = jnp.zeros((ny, LANES), jnp.float32)
     for lt in range(nl):
         FX[lt, nx] = zero_plane
+        FXR[lt, 0] = zero_plane
         FYR[lt] = zero_plane
         for k in range(ITERS):
             V[k, lt, 0, Y0 : Y0 + ny] = zero_plane
@@ -157,9 +160,7 @@
 
     x_low, x_high = gx > 0, gx < N_GX - 1
 
-    face_x = remote(
-        FX.at[:, pl.ds(0, 1)], FX.at[:, pl.ds(nx, 1)], face_send.at[0], face_recv.at[0], gx - 1, gy
-    )
+    face_x = remote(FX.at[:, pl.ds(0, 1)], FXR, face_send.at[0], face_recv.at[0], gx - 1, gy)
     face_y = remote(FYP, FYR, face_send.at[1], face_recv.at[1], gx, gy - 1)
     fy_flat = FY.reshape(nl, nx * 40, LANES)
 
@@ -211,19 +212,24 @@
             gx + 1,
             gy,
         )
-        down_y = remote(YP.at[k, 0], YR.at[k, 1], halo_send.at[k, 2], halo_recv.at[k, 2], gx, gy - 1)
-        up_y = remote(YP.at[k, 1], YR.at[k, 0], halo_send.at[k, 3], halo_recv.at[k, 3], gx, gy + 1)
+        row_0, row_1 = (YX.at[k, side, :, pl.ds(8, nx)] for side in range(2))
+        down_y = remote(row_0, YR.at[k, 1], halo_send.at[k, 2], halo_recv.at[k, 2], gx, gy - 1)
+        up_y = remote(row_1, YR.at[k, 0], halo_send.at[k, 3], halo_recv.at[k, 3], gx, gy + 1)
         return down_x, up_x, down_y, up_y
 
     halos = [halo_copies(k) for k in range(ITERS)]
 
-    def send_y(k):
+    def send_low_x(k):
+        guarded(x_low, halos[k][0].start)
+
+    def send_high_x(k):
+        guarded(x_high, halos[k][1].start)
+
+    def send_low_y(k):
         guarded(has_down, halos[k][2].start)
+
+    def send_high_y(k):
         guarded(has_up, halos[k][3].start)
-
-    def send_x(k):
-        guarded(x_low, halos[k][0].start)
-        guarded(x_high, halos[k][1].start)
 
     def wait_halo(k):
         down_x, up_x, down_y, up_y = halos[k]
@@ -235,6 +241,18 @@
         guarded(has_up, down_y.wait_recv)
         guarded(has_up, up_y.wait_send)
         guarded(has_down, up_y.wait_recv)
+
+    def insert_ends(k):
+        for lt in range(nl):
+            for x in (0, nx - 1):
+                at = pl.ds(x, 1)
+                V[k, lt, x + 1, pl.ds(Y0 - 1, 1), :] = YR[k, 0, lt, at, :]
+                V[k, lt, x + 1, pl.ds(Y0 + ny, 1), :] = YR[k, 1, lt, at, :]
+            for side, y in ((0, 0), (1, ny - 1)):
+                YX[k, side, lt, pl.ds(7, 1), :] = V[k, lt, 0, pl.ds(Y0 + y, 1), :]
+                YX[k, side, lt, pl.ds(8 + nx, 1), :] = V[k, lt, nx + 1, pl.ds(Y0 + y, 1), :]
+
+    def insert_rows(k):
         for lt in range(nl):
             v_flat[k, lt, pl.ds(48 + Y0 - 1, nx, stride=48), :] = YR[k, 0, lt]
             v_flat[k, lt, pl.ds(48 + Y0 + ny, nx, stride=48), :] = YR[k, 1, lt]
@@ -292,34 +310,47 @@
 
         return body
 
-    flat = {n: r.reshape(nl, nx * ny, LANES) for n, r in (("b", B), ("z", FZ), ("zu", FZU), ("inv", INV))}
     fx_flat = FX.reshape(nl, (nx + 1) * ny, LANES)
-
-    def edge_rows(k, c1, c2):
+    b_flat, dg_flat, fz_flat, fzu_flat, inv_flat = (
+        ref.reshape(nl, nx * ny, LANES) for ref in (B, DG, FZ, FZU, INV)
+    )
+
+    def pack_edges():
         for side, y in ((0, 0), (1, ny - 1)):
-            for j in range(nx // 8):
-
-                def v_row(kk, lt, dx, dy):
-                    return v_flat[
-                        kk, lt, pl.ds((1 + 8 * j + dx) * 48 + Y0 + y + dy, 8, stride=48), :
-                    ]
-
-                def row(ref, lt, dx=0):
-                    return ref[lt, pl.ds((8 * j + dx) * ny + y, 8, stride=ny), :]
-
-                c = [v_row(k, lt, 0, 0) for lt in range(nl)]
-                low, high = z_lower(c), z_upper(c)
-                for lt in range(nl):
-                    t = row(flat["b"], lt) + row(fx_flat, lt) * v_row(k, lt, -1, 0)
-                    t = t + row(fx_flat, lt, 1) * v_row(k, lt, 1, 0)
-                    at = 8 * j * 40 + y
-                    t = t + fy_flat[lt, pl.ds(at, 8, stride=40), :] * v_row(k, lt, 0, -1)
-                    t = t + fy_flat[lt, pl.ds(at + 1, 8, stride=40), :] * v_row(k, lt, 0, 1)
-                    t = t + row(flat["z"], lt) * low[lt] + row(flat["zu"], lt) * high[lt]
-                    new = (1.0 + c1 - c2) * c[lt] + c2 * (row(flat["inv"], lt) * t)
-                    if k > 0:
-                        new = new - c1 * v_row(k - 1, lt, 0, 0)
-                    YP[k + 1, side, lt, 8 * j : 8 * j + 8] = new
+            for lt in range(nl):
+                own, above = pl.ds(y, nx, stride=ny), pl.ds(ny + y, nx, stride=ny)
+                EC[0, side, lt] = b_flat[lt, own, :]
+                EC[1, side, lt] = fx_flat[lt, own, :]
+                EC[2, side, lt] = fx_flat[lt, above, :]
+                EC[3, side, lt] = fy_flat[lt, pl.ds(y, nx, stride=40), :]
+                EC[4, side, lt] = fy_flat[lt, pl.ds(y + 1, nx, stride=40), :]
+                EC[5, side, lt] = fz_flat[lt, own, :]
+                EC[6, side, lt] = fzu_flat[lt, own, :]
+                EC[7, side, lt] = inv_flat[lt, own, :]
+
+    def edge_rows(k, c1, c2, side):
+        inner = 1 if side == 0 else ny - 2
+        for j in range(nx // 8):
+            rows = pl.ds(8 * j, 8)
+            c = [YX[k, side, lt, pl.ds(8 + 8 * j, 8), :] for lt in range(nl)]
+            low, high = z_lower(c), z_upper(c)
+            for lt in range(nl):
+
+                def coef(i):
+                    return EC[i, side, lt, rows, :]
+
+                beyond = YR[k, side, lt, rows, :]
+                within = v_flat[k, lt, pl.ds((1 + 8 * j) * 48 + Y0 + inner, 8, stride=48), :]
+                y_low, y_high = (beyond, within) if side == 0 else (within, beyond)
+                t = coef(0) + coef(1) * YX[k, side, lt, pl.ds(7 + 8 * j, 8), :]
+                t = t + coef(2) * YX[k, side, lt, pl.ds(9 + 8 * j, 8), :]
+                t = t + coef(3) * y_low
+                t = t + coef(4) * y_high
+                t = t + coef(5) * low[lt] + coef(6) * high[lt]
+                new = (1.0 + c1 - c2) * c[lt] + c2 * (coef(7) * t)
+                if k > 0:
+                    new = new - c1 * YX[k - 1, side, lt, pl.ds(8 + 8 * j, 8), :]
+                YX[k + 1, side, lt, pl.ds(8 + 8 * j, 8), :] = new
 
     row_i = lax.broadcasted_iota(jnp.int32, (LANES, LANES), 0)
     col_i = lax.broadcasted_iota(jnp.int32, (LANES, LANES), 1)
@@ -446,16 +477,14 @@
         return pltpu.make_async_copy(S2.at[f, gx], landing(f), two_local.at[f])
 
     def start_two(f):
-        def pack(o, carry):
+        @pl.loop(0, N_GX - 1)
+        def _(i):
+            d = lax.rem(i + 5, N_GX - 1) + 1
+            o = lax.rem(gx + d, N_GX)
             S2[f, o] = spread[f][box_of[o]]
-            return carry
-
-        lax.fori_loop(0, N_GX, pack, 0, unroll=4)
-
-        @pl.loop(1, N_GX)
-        def _(d):
             two_copy(f, d).start()
 
+        S2[f, gx] = spread[f][box_of[gx]]
         two_own(f).start()
 
     def wait_two(f):
@@ -467,11 +496,16 @@
 
     def advance(k):
         body = sweep(k, *steps[k])
+        insert_ends(k)
         body(0, (0, 1, 2, 3))
+        send_low_x(k + 1)
         body(nx - 1, (0, 1, 2, 3))
-        send_x(k + 1)
-        edge_rows(k, *steps[k])
-        send_y(k + 1)
+        send_high_x(k + 1)
+        edge_rows(k, *steps[k], 0)
+        send_low_y(k + 1)
+        edge_rows(k, *steps[k], 1)
+        send_high_y(k + 1)
+        insert_rows(k)
         planes(body, 1, nx - 1, (0, 1, 2, 3), 5)
 
     def restrict_y():
@@ -490,24 +524,37 @@
     start_one(2)
     for which in (2, 3, 4):
         wait_load(which)
-    planes(first, 0, nx - 1, (0, 1, 2), 2)
+    for lt in range(nl):
+        fy_flat[lt, pl.ds(ny, nx, stride=40), :] = zero_plane
+    planes(first, 0, nx, (0, 1, 2, 3), 4)
     guarded(x_high, face_x.wait_recv)
     guarded(x_low, face_x.wait_send)
     guarded(has_up, face_y.wait_recv)
     guarded(has_down, face_y.wait_send)
     for lt in range(nl):
+        FX[lt, nx] = FXR[lt, 0]
         fy_flat[lt, pl.ds(ny, nx, stride=40), :] = FYR[lt]
-    first(nx - 1, (0, 1, 2))
-    planes(first, 0, nx, (3,), 4)
-    send_x(0)
+        last_row = pl.ds(ny - 1, nx, stride=ny)
+        d = dg_flat[lt, last_row, :] + FYR[lt]
+        inv = 1.0 / d
+        dg_flat[lt, last_row, :] = d
+        inv_flat[lt, last_row, :] = inv
+        v_flat[0, lt, pl.ds(48 + Y0 + ny - 1, nx, stride=48), :] = (
+            inv * b_flat[lt, last_row, :] * (1.0 / theta)
+        )
+    first(nx - 1, (0, 1, 2, 3))
+    send_low_x(0)
+    send_high_x(0)
     for lt in range(nl):
-        YP[0, 0, lt] = v_flat[0, lt, pl.ds(48 + Y0, nx, stride=48), :]
-        YP[0, 1, lt] = v_flat[0, lt, pl.ds(48 + Y0 + ny - 1, nx, stride=48), :]
-    send_y(0)
+        YX[0, 0, lt, 8 : 8 + nx] = v_flat[0, lt, pl.ds(48 + Y0, nx, stride=48), :]
+        YX[0, 1, lt, 8 : 8 + nx] = v_flat[0, lt, pl.ds(48 + Y0 + ny - 1, nx, stride=48), :]
+    send_low_y(0)
+    send_high_y(0)
     restrict(3, four(FZ), 0.25, True)
     start_one(3)
     restrict(0, four(AL), 0.125, False)
     start_one(0)
+    pack_edges()
     wait_halo(0)
     advance(0)
     restrict_x()
@@ -543,6 +590,7 @@
 
     planes(last, 1, 15, (1, 2), 2)
     wait_halo(3)
+    insert_rows(3)
     last(0, (0, 1, 2, 3))
     planes(last, 1, 8, (0, 3), 7)
     restrict_residual(0, 8)
@@ -559,6 +607,19 @@
     start_two(4)
     for f in range(5):
         wait_two(f)
+
+
+def write_out(sol_ref, cres_ref, ccoef_ref, sol_hbm, cres_hbm, ccoef_hbm, sem):
+    copies = []
+    for i in range(4):
+        part = pl.ds(8 * i, 8)
+        copies.append(pltpu.make_async_copy(sol_ref.at[part], sol_hbm.at[part], sem.at[i]))
+    copies.append(pltpu.make_async_copy(ccoef_ref, ccoef_hbm, sem.at[4]))
+    copies.append(pltpu.make_async_copy(cres_ref, cres_hbm, sem.at[5]))
+    for c in copies:
+        c.start()
+    for c in copies:
+        c.wait()
 
 
 def local(n_gy, right_side, alpha_coef, face_coef, owner_map):
@@ -588,10 +649,12 @@
             cells,
             vmem((ITERS, 4, 34, 48, LANES), f32),
             vmem((4, 16, 32, LANES), f32),
+            vmem((ITERS, 2, 4, 48, LANES), f32),
             vmem((ITERS, 2, 4, 32, LANES), f32),
-            vmem((ITERS, 2, 4, 32, LANES), f32),
+            vmem((8, 2, 4, 32, LANES), f32),
             vmem((4, 32, LANES), f32),
             vmem((4, 32, LANES), f32),
+            vmem((4, 1, 32, LANES), f32),
             vmem((4, 256, LANES), f32),
             vmem((2, 16, 16, LANES), f32),
             vmem((5, 4, 4, 4, 8, LANES), f32),
@@ -615,7 +678,16 @@
         ),
         name="smooth_and_restrict",
     )(owner_map, right_side, alpha_coef, face_coef)
-    return sol, cres, ccoef
+    arrays = (sol, cres, ccoef)
+    return pl.pallas_call(
+        write_out,
+        out_shape=tuple(jax.ShapeDtypeStruct(x.shape, f32) for x in arrays),
+        in_specs=[on_chip] * 3,
+        out_specs=(hbm,) * 3,
+        scratch_shapes=[dma((6,))],
+        compiler_params=pltpu.CompilerParams(vmem_limit_bytes=1 << 20),
+        name="write_out",
+    )(*arrays)
 
 
 def solution(mesh):

time: 59 us -> 57.2 us (0.969)
  local copies, waits for them, and re-layouts: 2.99 us -> 0 us
  Pallas kernels: 55.1 us -> 56.4 us
    unnamed x3 -> x0, local copies, waits for them, and re-layouts: 2.99 us -> none
    pallas_call x0 -> x1, Pallas kernels: none -> 1.79 us  [local(): pl.pallas_call(write_out, out_shape=tuple((jax.ShapeDtypeStruct(x.shape,...]
where the time goes in v3:
time: 57.2 us; the launch traced here: 57.1 us
  Pallas kernels  56.4 us (99%)
  between operations  0.64 us (1%)
    pallas_call x1, Pallas kernels, local(): pl.pallas_call(functools.partial(kernel, n_gy), out_shape=(vmem((32, 32,...  54.6 us
    pallas_call x1, Pallas kernels, local(): pl.pallas_call(write_out, out_shape=tuple((jax.ShapeDtypeStruct(x.shape,...  1.79 us

profile of v3, /device:TPU:9, one launch (start us, length us, event | category | flops | bytes accessed | tf_op | source)
XLA Modules:
  0.0 57.1 jit_solution(9758373675756902808)
XLA Ops:
  0.6 54.6 %smooth_and_restrict.1 = (f32[32,32,512]{2,1,0:T(8,128)S(1)}, f32[16,16,256]{2,1,0:T(8,128)S(1)}, f32[4,16,16,256]{3,2,1,0:T(8,128)S(1)}) custom-call(s32[1,256]{1,0:T(1,128)} %owner_ref.1, f32[32,32,512]{2,1,0:T(8,128)} %b_hbm.1, f32[32,32,512]{2,1,0:T(8,128)} %alpha_hbm.1, f32[3,32,32,512]{3,2,1,0:T(8,128)} %face_hbm.1), custom_call_target="tpu_custom_call" | custom-call | tf_op jit(solution)/shard_map/smooth_and_restrict/pallas_call | solution.py:632
  55.3 1.8 %write_out.1 = (f32[32,32,512]{2,1,0:T(8,128)}, f32[16,16,256]{2,1,0:T(8,128)}, f32[4,16,16,256]{3,2,1,0:T(8,128)}) custom-call(f32[32,32,512]{2,1,0:T(8,128)S(1)} %get-tuple-element.6.sol_ref, f32[16,16,256]{2,1,0:T(8,128)S(1)} %get-tuple-element.7.cres_ref, f32[4,16,16,256]{3,2,1,0:T(8,128)S(1)} %get-tuple-element.8.ccoef_ref), custom_call_target="tpu_custom_call" | custom-call | tf_op jit(solution)/shard_map/write_out/pallas_call | solution.py:682

commit v4 on v3

--- a/solution.py
+++ b/solution.py
@@ -114,6 +114,11 @@
             YR[k, 0, lt] = zero_plane
             YR[k, 1, lt] = zero_plane
 
+    v_flat = V.reshape(ITERS, nl, (nx + 2) * 48, LANES)
+    for lt in range(nl):
+        v_flat[ITERS - 1, lt, pl.ds(48 + Y0 - 1, nx, stride=48), :] = zero_plane
+        v_flat[ITERS - 1, lt, pl.ds(48 + Y0 + ny, nx, stride=48), :] = zero_plane
+
     barrier = pltpu.get_barrier_semaphore()
 
     @pl.loop(1, N_GX)
@@ -191,8 +196,6 @@
             jnp.where(last_lane, turned[i + 1] if i < nl - 1 else blank, turned[i])
             for i in range(nl)
         ]
-
-    v_flat = V.reshape(ITERS, nl, (nx + 2) * 48, LANES)
 
     def halo_copies(k):
         rows = pl.ds(Y0, ny)
@@ -279,15 +282,18 @@
                 INV[lt, x, rows, :] = inv
                 V[0, lt, x + 1, pl.ds(Y0 + 8 * yt, 8), :] = inv * B[lt, x, rows, :] * (1.0 / theta)
 
-    def gathered(k, x, yt):
+    def gathered(k, x, yt, low_x=True, high_x=True):
         rows = pl.ds(8 * yt, 8)
         y = Y0 + 8 * yt
         c = [V[k, lt, x + 1, pl.ds(y, 8), :] for lt in range(nl)]
         low, high = z_lower(c), z_upper(c)
         t = []
         for lt in range(nl):
-            s = B[lt, x, rows, :] + FX[lt, x, rows, :] * V[k, lt, x, pl.ds(y, 8), :]
-            s = s + FX[lt, x + 1, rows, :] * V[k, lt, x + 2, pl.ds(y, 8), :]
+            s = B[lt, x, rows, :]
+            if low_x:
+                s = s + FX[lt, x, rows, :] * V[k, lt, x, pl.ds(y, 8), :]
+            if high_x:
+                s = s + FX[lt, x + 1, rows, :] * V[k, lt, x + 2, pl.ds(y, 8), :]
             s = s + FY[lt, x, rows, :] * V[k, lt, x + 1, pl.ds(y - 1, 8), :]
             s = s + FY[lt, x, pl.ds(8 * yt + 1, 8), :] * V[k, lt, x + 1, pl.ds(y + 1, 8), :]
             s = s + FZ[lt, x, rows, :] * low[lt] + FZU[lt, x, rows, :] * high[lt]
@@ -356,13 +362,19 @@
     col_i = lax.broadcasted_iota(jnp.int32, (LANES, LANES), 1)
     groups = [(lane // 16) // d % 2 == 1 for d in (4, 2, 1)]
 
-    def restrict(f, pairs, weight, even_only, first_x=0, last_x=16):
+    def gather_pairs(pairs):
         def gather(X, carry):
             for lt in range(nl):
                 SB[lt, pl.ds(pl.multiple_of(X * 16, 16), 16), :] = pairs(lt, X)
             return carry
 
-        lax.fori_loop(first_x, last_x, gather, 0, unroll=4)
+        lax.fori_loop(0, 16, gather, 0, unroll=4)
+
+    def restrict(f, pairs, weight, even_only):
+        gather_pairs(pairs)
+        to_tiles(f, weight, even_only)
+
+    def to_tiles(f, weight, even_only):
         for half in range(2):
             total = None
             for side in range(2):
@@ -370,17 +382,17 @@
                 if even_only:
                     hit = hit & (row_i % 2 == 0)
                 pick = jnp.where(hit, weight, 0.0).astype(jnp.float32).astype(jnp.bfloat16)
-                rest = SB[2 * half + side, first_x * 16 : last_x * 16]
+                rest = SB[2 * half + side]
                 for _ in range(3):
                     piece = rest.astype(jnp.bfloat16)
                     rest = rest - piece.astype(jnp.float32)
                     part = jnp.dot(piece, pick, preferred_element_type=jnp.float32)
                     total = part if total is None else total + part
-            CB[half, first_x:last_x] = total.reshape(last_x - first_x, 16, LANES)
+            CB[half] = total.reshape(16, 16, LANES)
 
         for half in range(2):
             for yt in range(2):
-                for xt in range(first_x // 8, last_x // 8):
+                for xt in range(2):
                     a = [CB[half, xt * 8 + j, 8 * yt : 8 * yt + 8, :] for j in range(8)]
                     for d, odd in zip((4, 2, 1), groups):
                         b = list(a)
@@ -567,40 +579,41 @@
     start_two(3)
     wait_halo(2)
     advance(2)
-    wait_one(0)
-    start_two(0)
-
-    def last(X, tiles):
+
+    def last(X, tiles, low_x=True, high_x=True):
         for yt_ in tiles:
             rows = pl.ds(8 * yt_, 8)
             acc = None
             for a in range(2):
                 x = 2 * X + a
-                t, c = gathered(3, x, yt_)
+                t, c = gathered(3, x, yt_, low_x or a == 1, high_x or a == 0)
                 res = [t[lt] - DG[lt, x, rows, :] * c[lt] for lt in range(nl)]
                 acc = res if acc is None else [p + q for p, q in zip(acc, res)]
             for lt in range(nl):
                 RES[lt, X, rows, :] = acc[lt]
 
-    def restrict_residual(lo, hi):
-        def pairs(lt, X):
-            return strided(RES, lt, X, 0) + strided(RES, lt, X, 1)
-
-        restrict(4, pairs, 0.125, False, lo, hi)
-
-    planes(last, 1, 15, (1, 2), 2)
+    planes(last, 1, 15, (0, 1, 2, 3), 2)
+    last(0, (0, 1, 2, 3), low_x=False)
+    last(15, (0, 1, 2, 3), high_x=False)
+    gather_pairs(lambda lt, X: strided(RES, lt, X, 0) + strided(RES, lt, X, 1))
+    wait_one(0)
+    start_two(0)
     wait_halo(3)
-    insert_rows(3)
-    last(0, (0, 1, 2, 3))
-    planes(last, 1, 8, (0, 3), 7)
-    restrict_residual(0, 8)
-    start_residual(0)
-    start_residual(2)
-    planes(last, 8, 15, (0, 3), 7)
-    last(15, (0, 1, 2, 3))
-    restrict_residual(8, 16)
-    start_residual(1)
-    start_residual(3)
+    rows = pl.ds(Y0, ny)
+    for lt in range(nl):
+        RES[lt, 0] = EC[3, 0, lt] * YR[3, 0, lt]
+        RES[lt, 1] = EC[4, 1, lt] * YR[3, 1, lt]
+        RES[lt, 2] = FX[lt, 0] * V[3, lt, 0, rows, :]
+        RES[lt, 3] = FX[lt, nx] * V[3, lt, nx + 1, rows, :]
+    for lt in range(nl):
+        for i, cells_ in enumerate((pl.ds(0, 16, stride=16), pl.ds(15, 16, stride=16))):
+            SB[lt, cells_, :] = SB[lt, cells_, :] + (strided(RES, lt, i, 0) + strided(RES, lt, i, 1))
+    for lt in range(nl):
+        for i, cells_ in ((2, pl.ds(0, 16)), (3, pl.ds(240, 16))):
+            SB[lt, cells_, :] = SB[lt, cells_, :] + (strided(RES, lt, i, 0) + strided(RES, lt, i, 1))
+    to_tiles(4, 0.125, False)
+    for q in range(4):
+        start_residual(q)
     wait_one(1)
     start_two(1)
     wait_residual()

time: 57.2 us -> 55.9 us (0.977)
  Pallas kernels: 56.4 us -> 54.7 us
    pallas_call x1, Pallas kernels: 54.6 us -> 53 us  [local(): pl.pallas_call(functools.partial(kernel, n_gy), out_shape=(vmem((32, 32,...]
where the time goes in v4:
time: 55.9 us; the launch traced here: 55.4 us
  Pallas kernels  54.7 us (98%)
  between operations  0.64 us (1%)
    pallas_call x1, Pallas kernels, local(): pl.pallas_call(functools.partial(kernel, n_gy), out_shape=(vmem((32, 32,...  53 us
    pallas_call x1, Pallas kernels, local(): pl.pallas_call(write_out, out_shape=tuple((jax.ShapeDtypeStruct(x.shape,...  1.79 us

profile of v4, /device:TPU:9, one launch (start us, length us, event | category | flops | bytes accessed | tf_op | source)
XLA Modules:
  0.0 55.4 jit_solution(3945977255143131018)
XLA Ops:
  0.6 53.0 %smooth_and_restrict.1 = (f32[32,32,512]{2,1,0:T(8,128)S(1)}, f32[16,16,256]{2,1,0:T(8,128)S(1)}, f32[4,16,16,256]{3,2,1,0:T(8,128)S(1)}) custom-call(s32[1,256]{1,0:T(1,128)} %owner_ref.1, f32[32,32,512]{2,1,0:T(8,128)} %b_hbm.1, f32[32,32,512]{2,1,0:T(8,128)} %alpha_hbm.1, f32[3,32,32,512]{3,2,1,0:T(8,128)} %face_hbm.1), custom_call_target="tpu_custom_call" | custom-call | tf_op jit(solution)/shard_map/smooth_and_restrict/pallas_call | solution.py:645
  53.6 1.8 %write_out.1 = (f32[32,32,512]{2,1,0:T(8,128)}, f32[16,16,256]{2,1,0:T(8,128)}, f32[4,16,16,256]{3,2,1,0:T(8,128)}) custom-call(f32[32,32,512]{2,1,0:T(8,128)S(1)} %get-tuple-element.6.sol_ref, f32[16,16,256]{2,1,0:T(8,128)S(1)} %get-tuple-element.7.cres_ref, f32[4,16,16,256]{3,2,1,0:T(8,128)S(1)} %get-tuple-element.8.ccoef_ref), custom_call_target="tpu_custom_call" | custom-call | tf_op jit(solution)/shard_map/write_out/pallas_call | solution.py:695
